TPU v7x, 256 devices: a whole 4x4x8 slice. The times are simulated.
256 devices in a mesh: grp: 16 (over x, y), ln: 16 (over z, core).
Axes of the slice: x: 4, y: 4, z: 8, core: 2. Of those that a mesh axis runs over, the one named last changes fastest.
Arguments:
- object_field: float32 [2, 2, 2048, 2048], P(None, None, ('grp', 'ln')), may hold values from -6 to 6
- probe_wave: float32 [2, 128, 128], replicated, may hold values from -6 to 6
- measured: float32 [2, 1024, 128, 128], P(None, ('grp', 'ln')), may hold values from 0.1 to 3
- positions: int32 [2, 1024], P(None, 'grp'), may hold values from 0 to 2047
- shear_steps: int32 [2, 2048], P(None, ('grp', 'ln')), may hold values from -64 to 64
- smooth_weight: float32 [2048, 2048], P(('grp', 'ln')), may hold values from 0.05 to 0.24
Outputs:
- smoothed_step: float32 [2, 2, 2048, 2048], P(None, None, ('grp', 'ln'))
Inputs may be any that keep to these rules, and one draw needn't show every extreme that they name: `positions`: a tile takes 128 columns from its first one on, wrapping around past the last column.
All inputs are finite; a program needn't handle non-finite values.
Results may differ from a plain program's by a relative error of at most 0.007.
Values may be sent and summed in bfloat16 or wider, within the bound.
No kernel may reach another device: no remote copies, remote signals or barrier semaphores. Data moves between devices by JAX's collectives and lax.ppermute only.
A program may use at most 64 MiB of HBM per device.

v0:
```python
import functools
import math

import jax
import jax.numpy as jnp
import numpy as np
from jax import lax
from jax.experimental import pallas as pl
from jax.experimental.pallas import tpu as pltpu
from jax.sharding import PartitionSpec as P

AMP_FLOOR = 0.25
FRESNEL = 100.0
SHEAR_UNITS = 8
LANES = 128
OUTER = 16
COLS = OUTER * LANES
ROWS = 8
BF16 = jnp.bfloat16
F32 = jnp.float32


def split_table(table):
    high = np.asarray(table, np.float32).astype(BF16)
    low = (np.asarray(table) - high.astype(np.float64)).astype(np.float32).astype(BF16)
    return np.stack([high, low])


def right_block(matrix):
    top = np.concatenate([matrix.real, matrix.imag], 1)
    bottom = np.concatenate([-matrix.imag, matrix.real], 1)
    return np.concatenate([top, bottom], 0)


def tables():
    counter = np.arange(LANES)
    signed = (counter + LANES // 2) % LANES - LANES // 2
    dft = np.exp(-2j * math.pi / LANES * (counter[:, None] * counter[None, :] % LANES))
    dft = dft / math.sqrt(LANES)
    step = np.exp(-1j * FRESNEL / LANES**2 * signed.astype(np.float64) ** 2)
    spread = (dft.conj() * step[None, :]) @ dft
    fourier = right_block(dft)
    fresnel = right_block(spread)
    return np.stack([split_table(t) for t in (fourier, fourier.T, fresnel, fresnel.T)])


def twiddles():
    turn = np.arange(OUTER)[:, None] * np.arange(LANES)[None, :]
    angle = 2.0 * math.pi / COLS * turn
    return np.stack([np.cos(angle), np.sin(angle)]).astype(np.float32)


def const_mul(value, angle_num, angle_den, sign):
    re, im = value
    eighth = 8 * angle_num / angle_den
    if eighth == 0:
        return value
    if eighth == 2:
        return (-im * sign, re * sign) if sign in (1, -1) else None
    cosine = math.cos(2.0 * math.pi * angle_num / angle_den)
    sine = sign * math.sin(2.0 * math.pi * angle_num / angle_den)
    return (re * cosine - im * sine, re * sine + im * cosine)


def small_dft(values, sign):
    count = len(values)
    if count == 1:
        return values
    even = small_dft(values[::2], sign)
    odd = small_dft(values[1::2], sign)
    out = [None] * count
    for k in range(count // 2):
        re, im = const_mul(odd[k], k, count, sign)
        out[k] = (even[k][0] + re, even[k][1] + im)
        out[k + count // 2] = (even[k][0] - re, even[k][1] - im)
    return out


def cmul(a, b):
    return (a[0] * b[0] - a[1] * b[1], a[0] * b[1] + a[1] * b[0])


def conj_mul(a, b):
    return (a[0] * b[0] + a[1] * b[1], a[0] * b[1] - a[1] * b[0])


def halves(x):
    high = x.astype(BF16)
    return high, (x - high.astype(F32)).astype(BF16)


def dot(a, b):
    return jnp.dot(a, b, preferred_element_type=F32)


def rmul(x, table, which):
    high, low = halves(x)
    top = table[which, 0]
    return dot(high, top) + (dot(low, top) + dot(high, table[which, 1]))


def lmul(table, which, x):
    high, low = halves(x)
    top = table[which, 0]
    return dot(top, high) + (dot(top, low) + dot(table[which, 1], high))


def shear_factors(shear, tilt):
    row = lax.broadcasted_iota(jnp.int32, (ROWS, LANES), 0)
    lane = lax.broadcasted_iota(jnp.int32, (ROWS, LANES), 1)
    steps = jnp.zeros((ROWS, LANES), jnp.int32)
    for r in range(ROWS):
        steps = jnp.where(row == r, shear[tilt, r], steps)
    units = SHEAR_UNITS * COLS

    def turn(count):
        count = jnp.bitwise_and(count, units - 1)
        count = jnp.where(count >= units // 2, count - units, count)
        angle = (-2.0 * math.pi / units) * count.astype(F32)
        return (jnp.cos(angle), jnp.sin(angle))

    freq = OUTER * lane - jnp.where(lane >= LANES // 2, COLS, 0)
    base = turn(freq * steps)
    first = turn(steps)
    powers = [(jnp.ones((ROWS, LANES), F32), jnp.zeros((ROWS, LANES), F32)), first]
    for i in range(2, OUTER):
        powers.append(cmul(powers[i // 2], powers[i - i // 2]))
    return base, powers


def put(ref, block, value):
    ref[block * ROWS : (block + 1) * ROWS, :LANES] = value[0]
    ref[block * ROWS : (block + 1) * ROWS, LANES:] = value[1]


def get(array, block):
    return (
        array[block * ROWS : (block + 1) * ROWS, :LANES],
        array[block * ROWS : (block + 1) * ROWS, LANES:],
    )


def forward_columns(chunks, tw, ref, base_block):
    mixed = small_dft(chunks, -1)
    for i in range(OUTER):
        w = (tw[0, i : i + 1, :], tw[1, i : i + 1, :])
        put(ref, base_block + i, conj_mul(w, mixed[i]))


def inverse_columns(array, base_block, tw):
    blocks = []
    for i in range(OUTER):
        w = (tw[0, i : i + 1, :] * (1.0 / OUTER), tw[1, i : i + 1, :] * (1.0 / OUTER))
        blocks.append(cmul(w, get(array, base_block + i)))
    return small_dft(blocks, 1)


def shear_kernel(shear, pos, obj, table, tw, out, x_ref, y_ref, z_ref, band):
    slices = obj.shape[0]
    tilts = band.shape[0]
    for s in range(slices):
        chunks = [
            tuple(obj[s, c, :, j * LANES : (j + 1) * LANES] for c in range(2)) for j in range(OUTER)
        ]
        forward_columns(chunks, tw, x_ref, s * OUTER)
    x_ref[...] = rmul(x_ref[...], table, 0)
    for t in range(tilts):
        base, powers = shear_factors(shear, t)
        for i in range(OUTER):
            phase = cmul(base, powers[i])
            for s in range(slices):
                put(y_ref, (t * slices + s) * OUTER + i, cmul(get(x_ref, s * OUTER + i), phase))
    z_ref[...] = rmul(y_ref[...], table, 1)
    for t in range(tilts):
        for s in range(slices):
            chunks = inverse_columns(z_ref, (t * slices + s) * OUTER, tw)
            for j in range(OUTER):
                for c in range(2):
                    row = (2 * s + c) * ROWS
                    band[t, row : row + ROWS, j * LANES : (j + 1) * LANES] = chunks[j][c]
                    if j == 0:
                        band[t, row : row + ROWS, COLS:] = chunks[j][c]
    depth = band.shape[1]
    lane = lax.broadcasted_iota(jnp.int32, (depth, LANES), 1)
    per_owner = out.shape[1] // tilts

    def owner(d, carry):
        for jj in range(per_owner):
            for t in range(tilts):
                p = pos[t, d * per_owner + jj]
                start = pl.multiple_of((p // LANES) * LANES, LANES)
                off = p % LANES
                back = (LANES - off) % LANES
                near = pltpu.roll(band[t, :, pl.ds(start, LANES)], back, 1)
                far = pltpu.roll(band[t, :, pl.ds(start + LANES, LANES)], back, 1)
                out[d, t * per_owner + jj] = jnp.where(lane < LANES - off, near, far).astype(BF16)
        return carry

    lax.fori_loop(0, out.shape[0], owner, 0)


def both(value, table, right, left):
    re, im = value
    tile = LANES
    half = rmul(jnp.concatenate([re, im], 1), table, right)
    stacked = jnp.concatenate(
        [
            jnp.concatenate([half[:tile, :tile], half[tile:, :tile]], 1),
            jnp.concatenate([half[:tile, tile:], half[tile:, tile:]], 1),
        ],
        0,
    )
    full = lmul(table, left, stacked)
    return (
        jnp.concatenate([full[:tile, :tile], full[:tile, tile:]], 0),
        jnp.concatenate([full[tile:, :tile], full[tile:, tile:]], 0),
    )


def tile_kernel(recv, measured, probe, table, out):
    owners = recv.shape[0]
    pair = recv.shape[1]
    parts = [[] for _ in range(4)]
    for p in range(pair):
        for d in range(owners):
            rows = recv[d, p].astype(F32)
            for k in range(4):
                parts[k].append(rows[k * ROWS : (k + 1) * ROWS])
    parts = [jnp.concatenate(part, 0) for part in parts]
    first, second = (parts[0], parts[1]), (parts[2], parts[3])
    start = tuple(jnp.concatenate([probe[c]] * pair, 0) for c in range(2))
    target = jnp.concatenate([measured[p] for p in range(pair)], 0)
    wave = both(cmul(start, first), table, 2, 3)
    far = both(cmul(wave, second), table, 0, 1)
    factor = 1.0 - target * lax.rsqrt(far[0] * far[0] + far[1] * far[1] + AMP_FLOOR)
    back = both((factor * far[0], factor * far[1]), table, 1, 0)
    grad1 = conj_mul(wave, back)
    back = both(conj_mul(second, back), table, 3, 2)
    grad0 = conj_mul(start, back)
    for p in range(pair):
        for d in range(owners):
            row = p * LANES + d * ROWS
            out[d, p] = jnp.concatenate(
                [g[row : row + ROWS] for g in (*grad0, *grad1)], 0
            ).astype(BF16)


def descent_kernel(shear, pos, recv, weight, table, tw, out, edges, acc, x_ref, y_ref):
    tilts = acc.shape[0]
    per_owner = recv.shape[1] // tilts
    depth = acc.shape[1]
    slices = depth // (2 * ROWS)
    acc[...] = jnp.zeros_like(acc)
    lane = lax.broadcasted_iota(jnp.int32, (depth, LANES), 1)

    def owner(d, carry):
        for jj in range(per_owner):
            for t in range(tilts):
                p = pos[t, d * per_owner + jj]
                start = pl.multiple_of((p // LANES) * LANES, LANES)
                off = p % LANES
                moved = pltpu.roll(recv[d, t * per_owner + jj].astype(F32), off, 1)
                here = lane >= off
                acc[t, :, pl.ds(start, LANES)] += jnp.where(here, moved, 0.0)
                acc[t, :, pl.ds(start + LANES, LANES)] += jnp.where(here, 0.0, moved)
        return carry

    lax.fori_loop(0, recv.shape[0], owner, 0)
    for t in range(tilts):
        for s in range(slices):
            chunks = []
            for j in range(OUTER):
                pair = []
                for c in range(2):
                    row = (2 * s + c) * ROWS
                    value = acc[t, row : row + ROWS, j * LANES : (j + 1) * LANES]
                    if j == 0:
                        value = value + acc[t, row : row + ROWS, COLS:]
                    pair.append(value)
                chunks.append(tuple(pair))
            forward_columns(chunks, tw, x_ref, (t * slices + s) * OUTER)
    x_ref[...] = rmul(x_ref[...], table, 0)
    for t in range(tilts):
        base, powers = shear_factors(shear, t)
        for i in range(OUTER):
            phase = cmul(base, powers[i])
            for s in range(slices):
                value = conj_mul(phase, get(x_ref, (t * slices + s) * OUTER + i))
                if t:
                    before = get(y_ref, s * OUTER + i)
                    value = (value[0] + before[0], value[1] + before[1])
                put(y_ref, s * OUTER + i, value)
    y_ref[...] = rmul(y_ref[...], table, 1)
    row = lax.broadcasted_iota(jnp.int32, (ROWS, LANES), 0)
    lane = lax.broadcasted_iota(jnp.int32, (ROWS, LANES), 1)
    for s in range(slices):
        chunks = inverse_columns(y_ref, s * OUTER, tw)
        for c in range(2):
            values = [chunk[c] for chunk in chunks]
            ahead = [pltpu.roll(v, 1, 1) for v in values]
            behind = [pltpu.roll(v, LANES - 1, 1) for v in values]
            for j in range(OUTER):
                v = values[j]
                cols = slice(j * LANES, (j + 1) * LANES)
                left = jnp.where(lane == 0, ahead[j - 1], ahead[j])
                right = jnp.where(lane == LANES - 1, behind[(j + 1) % OUTER], behind[j])
                above = jnp.where(row == 0, 0.0, pltpu.roll(v, 1, 0))
                below = jnp.where(row == ROWS - 1, 0.0, pltpu.roll(v, ROWS - 1, 0))
                around = (above + below) + (left + right)
                out[s, c, :, cols] = v + weight[:, cols] * (around - 4.0 * v)
                edges[0, 2 * s + c : 2 * s + c + 1, cols] = v[:1]
                edges[1, 2 * s + c : 2 * s + c + 1, cols] = v[ROWS - 1 :]


VMEM = pl.BlockSpec(memory_space=pltpu.VMEM)
SMEM = pl.BlockSpec(memory_space=pltpu.SMEM)


def per_device(object_field, probe_wave, measured, positions, shear_steps, smooth_weight):
    slices = object_field.shape[0]
    tilts, per_owner = measured.shape[:2]
    owners = lax.axis_size("ln")
    tiles = tilts * per_owner
    depth = 2 * slices * ROWS
    table = jnp.asarray(tables())
    tw = jnp.asarray(twiddles())
    rows = slices * OUTER * ROWS
    chunk = (owners, tiles, depth, LANES)
    send = pl.pallas_call(
        shear_kernel,
        out_shape=jax.ShapeDtypeStruct(chunk, BF16),
        in_specs=[SMEM, SMEM, VMEM, VMEM, VMEM],
        out_specs=VMEM,
        scratch_shapes=[
            pltpu.VMEM((rows, 2 * LANES), F32),
            pltpu.VMEM((tilts * rows, 2 * LANES), F32),
            pltpu.VMEM((tilts * rows, 2 * LANES), F32),
            pltpu.VMEM((tilts, depth, COLS + LANES), F32),
        ],
        name="shear",
    )(shear_steps, positions, object_field, table[:2], tw)
    recv = lax.all_to_all(send, "ln", 0, 0, tiled=True)
    pair = 2
    grads = pl.pallas_call(
        tile_kernel,
        out_shape=jax.ShapeDtypeStruct(chunk, BF16),
        grid=(tiles // pair,),
        in_specs=[
            pl.BlockSpec((owners, pair, depth, LANES), lambda g: (0, g, 0, 0)),
            pl.BlockSpec((pair, LANES, LANES), lambda g: (g, 0, 0)),
            pl.BlockSpec((2, LANES, LANES), lambda g: (0, 0, 0)),
            pl.BlockSpec(table.shape, lambda g: (0, 0, 0, 0)),
        ],
        out_specs=pl.BlockSpec((owners, pair, depth, LANES), lambda g: (0, g, 0, 0)),
        name="tiles",
    )(recv, measured.reshape(tiles, LANES, LANES), probe_wave, table)
    back = lax.all_to_all(grads, "ln", 0, 0, tiled=True)
    partial, edges = pl.pallas_call(
        descent_kernel,
        out_shape=(
            jax.ShapeDtypeStruct((slices, 2, ROWS, COLS), F32),
            jax.ShapeDtypeStruct((2, 2 * slices, COLS), F32),
        ),
        in_specs=[SMEM, SMEM, VMEM, VMEM, VMEM, VMEM],
        out_specs=(VMEM, VMEM),
        scratch_shapes=[
            pltpu.VMEM((tilts, depth, COLS + LANES), F32),
            pltpu.VMEM((tilts * rows, 2 * LANES), F32),
            pltpu.VMEM((rows, 2 * LANES), F32),
        ],
        name="descent",
    )(shear_steps, positions, back, smooth_weight, table[:2], tw)
    count = lax.axis_size("grp") * owners
    above = lax.ppermute(edges[1], ("grp", "ln"), [(i, i + 1) for i in range(count - 1)])
    below = lax.ppermute(edges[0], ("grp", "ln"), [(i + 1, i) for i in range(count - 1)])
    shape = (slices, 2, 1, COLS)
    gap = jnp.zeros((slices, 2, ROWS - 2, COLS), F32)
    outside = jnp.concatenate([above.reshape(shape), gap, below.reshape(shape)], 2)
    return partial + smooth_weight * outside


def solution(mesh):
    in_specs = (
        P(None, None, ("grp", "ln"), None),
        P(),
        P(None, ("grp", "ln"), None, None),
        P(None, "grp"),
        P(None, ("grp", "ln")),
        P(("grp", "ln"), None),
    )
    out_specs = P(None, None, ("grp", "ln"), None)
    return jax.shard_map(
        per_device, mesh=mesh, in_specs=in_specs, out_specs=out_specs, check_vma=False
    )
```

profile of v0, /device:TPU:4, one launch (start us, length us, event | category | flops | bytes accessed | tf_op | source)
XLA Modules:
  0.0 105.0 jit_solution(8965583867096537640)
XLA Ops:
  0.0 5.4 %shear.3 = bf16[16,8,32,128]{3,2,1,0:T(8,128)(2,1)} custom-call(s32[2,8]{1,0:T(2,128)} %shear.5, s32[2,64]{1,0:T(2,128)} %pos.3, f32[2,2,8,2048]{3,2,1,0:T(8,128)} %obj.1, bf16[2,2,256,256]{3,2,1,0:T(8,128)(2,1)} %constant.12.table, f32[2,16,128]{2,1,0:T(8,128)} %constant.7.clone.tw), custom_call_target="tpu_custom_call" | custom-call | tf_op jit(solution)/shard_map/shear/pallas_call | solution.py:329
  5.4 35.8 %all_to_all.10.recv = bf16[16,8,32,128]{3,2,1,0:T(8,128)(2,1)} all-to-all(bf16[16,8,32,128]{3,2,1,0:T(8,128)(2,1)} %shear.3), channel_id=1, replica_groups=mesh['grp'=16,'ln'=16] {'ln'}, dimensions={0} | all-to-all | bytes 2097152 | tf_op jit(solution)/shard_map/all_to_all | solution.py:342
  41.2 12.7 %tiles.1 = bf16[16,8,32,128]{3,2,1,0:T(8,128)(2,1)} custom-call(bf16[16,8,32,128]{3,2,1,0:T(8,128)(2,1)} %all_to_all.10.recv, f32[8,128,128]{2,1,0:T(8,128)} %bitcast.5, f32[2,128,128]{2,1,0:T(8,128)} %probe.1, bf16[4,2,256,256]{3,2,1,0:T(8,128)(2,1)} %constant.6.clone.table), custom_call_target="tpu_custom_call" | custom-call | tf_op jit(solution)/shard_map/tiles/pallas_call | solution.py:344
  53.9 31.6 %all_to_all.11.recv = bf16[16,8,32,128]{3,2,1,0:T(8,128)(2,1)} all-to-all(bf16[16,8,32,128]{3,2,1,0:T(8,128)(2,1)} %tiles.1), channel_id=1, replica_groups=mesh['grp'=16,'ln'=16] {'ln'}, dimensions={0} | all-to-all | bytes 2097152 | tf_op jit(solution)/shard_map/all_to_all | solution.py:357
  85.5 5.5 %descent.1 = (f32[2,2,8,2048]{3,2,1,0:T(8,128)}, f32[2,4,2048]{2,1,0:T(4,128)}) custom-call(s32[2,8]{1,0:T(2,128)} %shear.5, s32[2,64]{1,0:T(2,128)} %pos.3, bf16[16,8,32,128]{3,2,1,0:T(8,128)(2,1)} %all_to_all.11.recv, f32[8,2048]{1,0:T(8,128)} %weight.1, bf16[2,2,256,256]{3,2,1,0:T(8,128)(2,1)} %constant.12.table, f32[2,16,128]{2,1,0:T(8,128)} %constant.7.clone.tw), custom_call_target="tpu_custom_call" | custom-call | tf_op jit(solution)/shard_map/descent/pallas_call | solution.py:358
  91.0 0.8 slice_bitcast_fusion.1
  91.8 3.6 %collective-permute-start = (f32[4,2048]{1,0:T(4,128)S(1)}, f32[4,2048]{1,0:T(4,128)S(1)}, u32[]{:S(2)}, u32[]{:S(2)}) collective-permute-start(f32[4,2048]{1,0:T(4,128)S(1)} %get-tuple-element.9), channel_id=1, source_target_pairs={{0,1},{1,2},{2,3},{3,4},{4,5},{5,6},{6,7},{7,8},{8,9},{9,10},{10,1... | collective-permute-start | bytes 98312 | tf_op jit(solution)/shard_map/ppermute | solution.py:374
  95.3 6.2 %collective-permute-start.1 = (f32[4,2048]{1,0:T(4,128)S(1)}, f32[4,2048]{1,0:T(4,128)S(1)}, u32[]{:S(2)}, u32[]{:S(2)}) collective-permute-start(f32[4,2048]{1,0:T(4,128)S(1)} %get-tuple-element.10), channel_id=1, source_target_pairs={{1,0},{2,1},{3,2},{4,3},{5,4},{6,5},{7,6},{8,7},{9,8},{10,9},{11,1... | collective-permute-start | bytes 98312 | tf_op jit(solution)/shard_map/ppermute | solution.py:375
  101.6 0.1 pad.1.clone
  101.6 0.0 copy-start
  101.6 0.0 collective-permute-done
  101.6 0.1 reshape.13
  101.7 1.4 %collective-permute-done.1 = f32[4,2048]{1,0:T(4,128)S(1)} collective-permute-done((f32[4,2048]{1,0:T(4,128)S(1)}, f32[4,2048]{1,0:T(4,128)S(1)}, u32[]{:S(2)}, u32[]{:S(2)}) %collective-permute-start.1) | collective-permute-done | bytes 32800 | tf_op jit(solution)/shard_map/ppermute | solution.py:375
  103.1 0.1 reshape.14
  103.2 0.0 copy-done
  103.2 1.8 %fusion = f32[2,2,8,2048]{3,2,1,0:T(8,128)} fusion(f32[2,2,8,2048]{3,2,1,0:T(8,128)} %get-tuple-element.7, f32[2,2,1,2048]{3,2,1,0:T(1,128)S(1)} %reshape.14, f32[2,2,1,2048]{3,2,1,0:T(1,128)S(1)} %reshape.13, f32[8]{0:T(128)S(1)} %pad.1.clone, f32[8,2048]{1,0:T(8,128)S(1)} %copy-done), kind=kLoop, calls=%fused_computation.1 | loop fusion | flops 262144 | bytes 655392 | tf_op jit(solution)/shard_map/add | solution.py:379
  (1 shorter events, 0.0 us)
Async XLA Ops:
  91.8 9.9 %collective-permute-start = (f32[4,2048]{1,0:T(4,128)S(1)}, f32[4,2048]{1,0:T(4,128)S(1)}, u32[]{:S(2)}, u32[]{:S(2)}) collective-permute-start(f32[4,2048]{1,0:T(4,128)S(1)} %get-tuple-element.9), channel_id=1, source_target_pairs={{0,1},{1,2},{2,3},{3,4},{4,5},{5,6},{6,7},{7,8},{8,9},{9,10},{10,1... | collective-permute-start | bytes 98312 | tf_op jit(solution)/shard_map/ppermute | solution.py:374
  95.3 7.8 %collective-permute-start.1 = (f32[4,2048]{1,0:T(4,128)S(1)}, f32[4,2048]{1,0:T(4,128)S(1)}, u32[]{:S(2)}, u32[]{:S(2)}) collective-permute-start(f32[4,2048]{1,0:T(4,128)S(1)} %get-tuple-element.10), channel_id=1, source_target_pairs={{1,0},{2,1},{3,2},{4,3},{5,4},{6,5},{7,6},{8,7},{9,8},{10,9},{11,1... | collective-permute-start | bytes 98312 | tf_op jit(solution)/shard_map/ppermute | solution.py:375
  101.6 1.5 %copy-start = (f32[8,2048]{1,0:T(8,128)S(1)}, f32[8,2048]{1,0:T(8,128)}, u32[]{:S(2)}) copy-start(f32[8,2048]{1,0:T(8,128)} %weight.1) | copy-start | bytes 196612
where the time goes:
time: 105 us
  blocking collectives  67.5 us (64%)
  Pallas kernels  23.5 us (22%)
  starting transfers between devices  9.77 us (9%)
  other arithmetic  1.77 us (2%)
  waiting for transfers between devices  1.43 us (1%)
    all_to_all x1, blocking collectives, per_device(): recv = lax.all_to_all(send, 'ln', 0, 0, tiled=True)  35.8 us
    all_to_all x1, blocking collectives, per_device(): back = lax.all_to_all(grads, 'ln', 0, 0, tiled=True)  31.6 us
    pallas_call x1, Pallas kernels, per_device(): pl.pallas_call(tile_kernel, out_shape=jax.ShapeDtypeStruct(chunk, BF16),...  12.7 us
    ppermute x1, starting transfers between devices, per_device(): lax.ppermute(edges[0], ('grp', 'ln'), [(i + 1, i) for i in range(count -...  6.2 us
    pallas_call x1, Pallas kernels, per_device(): pl.pallas_call(descent_kernel, out_shape=(jax.ShapeDtypeStruct((slices, 2...  5.46 us
    pallas_call x1, Pallas kernels, per_device(): pl.pallas_call(shear_kernel, out_shape=jax.ShapeDtypeStruct(chunk, BF16),...  5.39 us
    ppermute x1, starting transfers between devices, per_device(): lax.ppermute(edges[1], ('grp', 'ln'), [(i, i + 1) for i in range(count -...  3.57 us
  transfers between devices with their start and end apart: 2, of which 1 were waited for; matrix products, arithmetic and copies ran while one was open for 0% of the time, Pallas kernels for 0%

commit v1 on v0

--- a/solution.py
+++ b/solution.py
@@ -16,6 +16,7 @@
 OUTER = 16
 COLS = OUTER * LANES
 ROWS = 8
+UNROLL = 4
 BF16 = jnp.bfloat16
 F32 = jnp.float32
 
@@ -184,88 +185,108 @@
     lane = lax.broadcasted_iota(jnp.int32, (depth, LANES), 1)
     per_owner = out.shape[1] // tilts
 
-    def owner(d, carry):
-        for jj in range(per_owner):
-            for t in range(tilts):
-                p = pos[t, d * per_owner + jj]
-                start = pl.multiple_of((p // LANES) * LANES, LANES)
-                off = p % LANES
-                back = (LANES - off) % LANES
-                near = pltpu.roll(band[t, :, pl.ds(start, LANES)], back, 1)
-                far = pltpu.roll(band[t, :, pl.ds(start + LANES, LANES)], back, 1)
-                out[d, t * per_owner + jj] = jnp.where(lane < LANES - off, near, far).astype(BF16)
+    def some_owners(step, carry):
+        for o in range(UNROLL):
+            d = step * UNROLL + o
+            for jj in range(per_owner):
+                for t in range(tilts):
+                    p = pos[t, d * per_owner + jj]
+                    off = jnp.bitwise_and(p, LANES - 1)
+                    start = pl.multiple_of(p - off, LANES)
+                    back = jnp.bitwise_and(LANES - off, LANES - 1)
+                    near = pltpu.roll(band[t, :, pl.ds(start, LANES)], back, 1)
+                    far = pltpu.roll(band[t, :, pl.ds(start + LANES, LANES)], back, 1)
+                    window = jnp.where(lane < LANES - off, near, far)
+                    out[d, t * per_owner + jj] = window.astype(BF16)
         return carry
 
-    lax.fori_loop(0, out.shape[0], owner, 0)
-
-
-def both(value, table, right, left):
-    re, im = value
+    lax.fori_loop(0, out.shape[0] // UNROLL, some_owners, 0)
+
+
+def both(values, table, right, left):
     tile = LANES
-    half = rmul(jnp.concatenate([re, im], 1), table, right)
-    stacked = jnp.concatenate(
-        [
-            jnp.concatenate([half[:tile, :tile], half[tile:, :tile]], 1),
-            jnp.concatenate([half[:tile, tile:], half[tile:, tile:]], 1),
-        ],
-        0,
-    )
-    full = lmul(table, left, stacked)
-    return (
-        jnp.concatenate([full[:tile, :tile], full[:tile, tile:]], 0),
-        jnp.concatenate([full[tile:, :tile], full[tile:, tile:]], 0),
-    )
+    halved = [rmul(jnp.concatenate(value, 1), table, right) for value in values]
+    stacked = [
+        jnp.concatenate(
+            [
+                jnp.concatenate([half[:tile, :tile], half[tile:, :tile]], 1),
+                jnp.concatenate([half[:tile, tile:], half[tile:, tile:]], 1),
+            ],
+            0,
+        )
+        for half in halved
+    ]
+    full = [lmul(table, left, x) for x in stacked]
+    return [
+        (
+            jnp.concatenate([x[:tile, :tile], x[:tile, tile:]], 0),
+            jnp.concatenate([x[tile:, :tile], x[tile:, tile:]], 0),
+        )
+        for x in full
+    ]
 
 
 def tile_kernel(recv, measured, probe, table, out):
     owners = recv.shape[0]
-    pair = recv.shape[1]
-    parts = [[] for _ in range(4)]
-    for p in range(pair):
-        for d in range(owners):
-            rows = recv[d, p].astype(F32)
-            for k in range(4):
-                parts[k].append(rows[k * ROWS : (k + 1) * ROWS])
-    parts = [jnp.concatenate(part, 0) for part in parts]
-    first, second = (parts[0], parts[1]), (parts[2], parts[3])
-    start = tuple(jnp.concatenate([probe[c]] * pair, 0) for c in range(2))
-    target = jnp.concatenate([measured[p] for p in range(pair)], 0)
-    wave = both(cmul(start, first), table, 2, 3)
-    far = both(cmul(wave, second), table, 0, 1)
-    factor = 1.0 - target * lax.rsqrt(far[0] * far[0] + far[1] * far[1] + AMP_FLOOR)
-    back = both((factor * far[0], factor * far[1]), table, 1, 0)
-    grad1 = conj_mul(wave, back)
-    back = both(conj_mul(second, back), table, 3, 2)
-    grad0 = conj_mul(start, back)
-    for p in range(pair):
-        for d in range(owners):
-            row = p * LANES + d * ROWS
-            out[d, p] = jnp.concatenate(
-                [g[row : row + ROWS] for g in (*grad0, *grad1)], 0
-            ).astype(BF16)
-
-
-def descent_kernel(shear, pos, recv, weight, table, tw, out, edges, acc, x_ref, y_ref):
-    tilts = acc.shape[0]
+    pairs = recv.shape[1] // 2
+    first, second, target = [], [], []
+    for q in range(pairs):
+        parts = [[] for _ in range(4)]
+        for p in (2 * q, 2 * q + 1):
+            for d in range(owners):
+                rows = recv[d, p].astype(F32)
+                for k in range(4):
+                    parts[k].append(rows[k * ROWS : (k + 1) * ROWS])
+        parts = [jnp.concatenate(part, 0) for part in parts]
+        first.append((parts[0], parts[1]))
+        second.append((parts[2], parts[3]))
+        target.append(jnp.concatenate([measured[2 * q], measured[2 * q + 1]], 0))
+    start = tuple(jnp.concatenate([probe[c]] * 2, 0) for c in range(2))
+    wave = both([cmul(start, x) for x in first], table, 2, 3)
+    far = both([cmul(w, x) for w, x in zip(wave, second)], table, 0, 1)
+    changed = []
+    for (re, im), m in zip(far, target):
+        factor = 1.0 - m * lax.rsqrt(re * re + im * im + AMP_FLOOR)
+        changed.append((factor * re, factor * im))
+    back = both(changed, table, 1, 0)
+    grad1 = [conj_mul(w, b) for w, b in zip(wave, back)]
+    back = both([conj_mul(x, b) for x, b in zip(second, back)], table, 3, 2)
+    grad0 = [conj_mul(start, b) for b in back]
+    for q in range(pairs):
+        grads = (*grad0[q], *grad1[q])
+        for p in range(2):
+            for d in range(owners):
+                row = p * LANES + d * ROWS
+                mine = jnp.concatenate([g[row : row + ROWS] for g in grads], 0)
+                out[d, 2 * q + p] = mine.astype(BF16)
+
+
+def descent_kernel(shear, pos, recv, weight, table, tw, out, near, far, *scratch):
+    accs, (x_ref, y_ref) = scratch[:-2], scratch[-2:]
+    tilts = len(accs) // 2
     per_owner = recv.shape[1] // tilts
-    depth = acc.shape[1]
+    depth = accs[0].shape[0]
     slices = depth // (2 * ROWS)
-    acc[...] = jnp.zeros_like(acc)
+    for acc in accs:
+        acc[...] = jnp.zeros_like(acc)
     lane = lax.broadcasted_iota(jnp.int32, (depth, LANES), 1)
 
-    def owner(d, carry):
-        for jj in range(per_owner):
-            for t in range(tilts):
-                p = pos[t, d * per_owner + jj]
-                start = pl.multiple_of((p // LANES) * LANES, LANES)
-                off = p % LANES
-                moved = pltpu.roll(recv[d, t * per_owner + jj].astype(F32), off, 1)
-                here = lane >= off
-                acc[t, :, pl.ds(start, LANES)] += jnp.where(here, moved, 0.0)
-                acc[t, :, pl.ds(start + LANES, LANES)] += jnp.where(here, 0.0, moved)
+    def some_owners(step, carry):
+        for o in range(UNROLL):
+            d = step * UNROLL + o
+            for jj in range(per_owner):
+                for t in range(tilts):
+                    acc = accs[t + tilts * (jj % 2)]
+                    p = pos[t, d * per_owner + jj]
+                    off = jnp.bitwise_and(p, LANES - 1)
+                    start = pl.multiple_of(p - off, LANES)
+                    moved = pltpu.roll(recv[d, t * per_owner + jj].astype(F32), off, 1)
+                    here = lane >= off
+                    spread = [jnp.where(here, moved, 0.0), jnp.where(here, 0.0, moved)]
+                    acc[:, pl.ds(start, 2 * LANES)] += jnp.concatenate(spread, 1)
         return carry
 
-    lax.fori_loop(0, recv.shape[0], owner, 0)
+    lax.fori_loop(0, recv.shape[0] // UNROLL, some_owners, 0)
     for t in range(tilts):
         for s in range(slices):
             chunks = []
@@ -273,9 +294,11 @@
                 pair = []
                 for c in range(2):
                     row = (2 * s + c) * ROWS
-                    value = acc[t, row : row + ROWS, j * LANES : (j + 1) * LANES]
-                    if j == 0:
-                        value = value + acc[t, row : row + ROWS, COLS:]
+                    value = 0.0
+                    for acc in (accs[t], accs[t + tilts]):
+                        value = value + acc[row : row + ROWS, j * LANES : (j + 1) * LANES]
+                        if j == 0:
+                            value = value + acc[row : row + ROWS, COLS:]
                     pair.append(value)
                 chunks.append(tuple(pair))
             forward_columns(chunks, tw, x_ref, (t * slices + s) * OUTER)
@@ -293,6 +316,7 @@
     y_ref[...] = rmul(y_ref[...], table, 1)
     row = lax.broadcasted_iota(jnp.int32, (ROWS, LANES), 0)
     lane = lax.broadcasted_iota(jnp.int32, (ROWS, LANES), 1)
+    odd = lax.rem(lax.axis_index("ln"), 2) == 1
     for s in range(slices):
         chunks = inverse_columns(y_ref, s * OUTER, tw)
         for c in range(2):
@@ -308,12 +332,27 @@
                 below = jnp.where(row == ROWS - 1, 0.0, pltpu.roll(v, ROWS - 1, 0))
                 around = (above + below) + (left + right)
                 out[s, c, :, cols] = v + weight[:, cols] * (around - 4.0 * v)
-                edges[0, 2 * s + c : 2 * s + c + 1, cols] = v[:1]
-                edges[1, 2 * s + c : 2 * s + c + 1, cols] = v[ROWS - 1 :]
+                first, last = v[:1], v[ROWS - 1 :]
+                near[2 * s + c : 2 * s + c + 1, cols] = jnp.where(odd, first, last)
+                far[2 * s + c : 2 * s + c + 1, cols] = jnp.where(odd, last, first)
+
+
+def halo_kernel(partial, near, far, weight, out):
+    odd = lax.rem(lax.axis_index("ln"), 2) == 1
+    row = lax.broadcasted_iota(jnp.int32, weight.shape, 0)
+    near_row = jnp.where(odd, 0, ROWS - 1)
+    at_near = jnp.where(row == near_row, weight[...], 0.0)
+    at_far = jnp.where(row == ROWS - 1 - near_row, weight[...], 0.0)
+    for s in range(out.shape[0]):
+        for c in range(2):
+            k = 2 * s + c
+            halo = at_near * near[k : k + 1, :] + at_far * far[k : k + 1, :]
+            out[s, c] = partial[s, c] + halo
 
 
 VMEM = pl.BlockSpec(memory_space=pltpu.VMEM)
 SMEM = pl.BlockSpec(memory_space=pltpu.SMEM)
+PARAMS = pltpu.CompilerParams(vmem_limit_bytes=24 << 20)
 
 
 def per_device(object_field, probe_wave, measured, positions, shear_steps, smooth_weight):
@@ -337,46 +376,51 @@
             pltpu.VMEM((tilts * rows, 2 * LANES), F32),
             pltpu.VMEM((tilts, depth, COLS + LANES), F32),
         ],
+        compiler_params=PARAMS,
         name="shear",
     )(shear_steps, positions, object_field, table[:2], tw)
     recv = lax.all_to_all(send, "ln", 0, 0, tiled=True)
-    pair = 2
+    group = 4
     grads = pl.pallas_call(
         tile_kernel,
         out_shape=jax.ShapeDtypeStruct(chunk, BF16),
-        grid=(tiles // pair,),
+        grid=(tiles // group,),
         in_specs=[
-            pl.BlockSpec((owners, pair, depth, LANES), lambda g: (0, g, 0, 0)),
-            pl.BlockSpec((pair, LANES, LANES), lambda g: (g, 0, 0)),
+            pl.BlockSpec((owners, group, depth, LANES), lambda g: (0, g, 0, 0)),
+            pl.BlockSpec((group, LANES, LANES), lambda g: (g, 0, 0)),
             pl.BlockSpec((2, LANES, LANES), lambda g: (0, 0, 0)),
             pl.BlockSpec(table.shape, lambda g: (0, 0, 0, 0)),
         ],
-        out_specs=pl.BlockSpec((owners, pair, depth, LANES), lambda g: (0, g, 0, 0)),
+        out_specs=pl.BlockSpec((owners, group, depth, LANES), lambda g: (0, g, 0, 0)),
+        compiler_params=PARAMS,
         name="tiles",
     )(recv, measured.reshape(tiles, LANES, LANES), probe_wave, table)
     back = lax.all_to_all(grads, "ln", 0, 0, tiled=True)
-    partial, edges = pl.pallas_call(
+    edge = jax.ShapeDtypeStruct((2 * slices, COLS), F32)
+    whole = jax.ShapeDtypeStruct((slices, 2, ROWS, COLS), F32)
+    partial, near, far = pl.pallas_call(
         descent_kernel,
-        out_shape=(
-            jax.ShapeDtypeStruct((slices, 2, ROWS, COLS), F32),
-            jax.ShapeDtypeStruct((2, 2 * slices, COLS), F32),
-        ),
+        out_shape=(whole, edge, edge),
         in_specs=[SMEM, SMEM, VMEM, VMEM, VMEM, VMEM],
-        out_specs=(VMEM, VMEM),
-        scratch_shapes=[
-            pltpu.VMEM((tilts, depth, COLS + LANES), F32),
-            pltpu.VMEM((tilts * rows, 2 * LANES), F32),
-            pltpu.VMEM((rows, 2 * LANES), F32),
-        ],
+        out_specs=(VMEM, VMEM, VMEM),
+        scratch_shapes=[pltpu.VMEM((depth, COLS + LANES), F32) for _ in range(2 * tilts)]
+        + [pltpu.VMEM((tilts * rows, 2 * LANES), F32), pltpu.VMEM((rows, 2 * LANES), F32)],
+        compiler_params=PARAMS,
         name="descent",
     )(shear_steps, positions, back, smooth_weight, table[:2], tw)
     count = lax.axis_size("grp") * owners
-    above = lax.ppermute(edges[1], ("grp", "ln"), [(i, i + 1) for i in range(count - 1)])
-    below = lax.ppermute(edges[0], ("grp", "ln"), [(i + 1, i) for i in range(count - 1)])
-    shape = (slices, 2, 1, COLS)
-    gap = jnp.zeros((slices, 2, ROWS - 2, COLS), F32)
-    outside = jnp.concatenate([above.reshape(shape), gap, below.reshape(shape)], 2)
-    return partial + smooth_weight * outside
+    axes = ("grp", "ln")
+    between = [(i, i + 1) for i in range(1, count - 1, 2)]
+    far = lax.ppermute(far, axes, between + [(j, i) for i, j in between])
+    near = lax.ppermute(near, axes, [(i, i ^ 1) for i in range(count)])
+    return pl.pallas_call(
+        halo_kernel,
+        out_shape=whole,
+        in_specs=[VMEM] * 4,
+        out_specs=VMEM,
+        compiler_params=PARAMS,
+        name="halo",
+    )(partial, near, far, smooth_weight)
 
 
 def solution(mesh):

time: 105 us -> 94.2 us (0.90)
  Pallas kernels: 23.5 us -> 11.4 us
  starting transfers between devices: 9.77 us -> 5.21 us
  waiting for transfers between devices: 1.43 us -> 5.98 us
  local copies, waits for them, and re-layouts: 0.96 us -> 4.12 us
  other arithmetic: 1.77 us -> 0 us
    pallas_call x1, Pallas kernels: 12.7 us -> 6.07 us  [per_device(): pl.pallas_call(tile_kernel, out_shape=jax.ShapeDtypeStruct(chunk, BF16),...]
    ppermute x2, starting transfers between devices: 9.77 us -> 5.21 us  [the longest x1 3.45 us: per_device(): far = lax.ppermute(far, axes, between + [(j, i) for i, j in between])]
    ppermute x2, waiting for transfers between devices: 1.43 us -> 5.98 us  [the longest x1 5.98 us: per_device(): far = lax.ppermute(far, axes, between + [(j, i) for i, j in between])]
    unnamed x2 -> x26, local copies, waits for them, and re-layouts: 0.01 us -> 4.12 us
    pallas_call x1, Pallas kernels: 5.39 us -> 2.25 us  [per_device(): pl.pallas_call(shear_kernel, out_shape=jax.ShapeDtypeStruct(chunk, BF16),...]
    pallas_call x1 -> x2, Pallas kernels: 5.46 us -> 3.06 us  [the longest x1 2.31 us: per_device(): pl.pallas_call(descent_kernel, out_shape=(whole, edge, edge), in_specs=[S...]
    add x1 -> x0, other arithmetic: 1.77 us -> none  [per_device(): return partial + smooth_weight * outside]
where the time goes in v1:
time: 94.2 us; the launch traced here: 93.9 us
  blocking collectives  67 us (71%)
  Pallas kernels  11.4 us (12%)
  waiting for transfers between devices  5.98 us (6%)
  starting transfers between devices  5.21 us (6%)
  local copies, waits for them, and re-layouts  4.12 us (4%)
    all_to_all x1, blocking collectives, per_device(): recv = lax.all_to_all(send, 'ln', 0, 0, tiled=True)  35.7 us
    all_to_all x1, blocking collectives, per_device(): back = lax.all_to_all(grads, 'ln', 0, 0, tiled=True)  31.4 us
    pallas_call x1, Pallas kernels, per_device(): pl.pallas_call(tile_kernel, out_shape=jax.ShapeDtypeStruct(chunk, BF16),...  6.07 us
    ppermute x1, waiting for transfers between devices, per_device(): far = lax.ppermute(far, axes, between + [(j, i) for i, j in between])  5.98 us
    unnamed x26, local copies, waits for them, and re-layouts  4.12 us
    ppermute x1, starting transfers between devices, per_device(): far = lax.ppermute(far, axes, between + [(j, i) for i, j in between])  3.45 us
    pallas_call x1, Pallas kernels, per_device(): pl.pallas_call(descent_kernel, out_shape=(whole, edge, edge), in_specs=[S...  2.31 us
    pallas_call x1, Pallas kernels, per_device(): pl.pallas_call(shear_kernel, out_shape=jax.ShapeDtypeStruct(chunk, BF16),...  2.25 us
  transfers between devices with their start and end apart: 2, of which 1 were waited for; matrix products, arithmetic and copies ran while one was open for 0% of the time, Pallas kernels for 0%

profile of v1, /device:TPU:4, one launch (start us, length us, event | category | flops | bytes accessed | tf_op | source)
XLA Modules:
  0.0 93.9 jit_solution(2876752329085763649)
XLA Ops:
  0.0 0.0 copy-start
  0.0 1.0 %copy-done = bf16[2,2,256,256]{3,2,1,0:T(8,128)(2,1)S(1)} copy-done((bf16[2,2,256,256]{3,2,1,0:T(8,128)(2,1)S(1)}, bf16[2,2,256,256]{3,2,1,0:T(8,128)(2,1)}, u32[]{:S(2)}) %copy-start) | copy-done | bytes 524312
  1.0 0.0 copy-start.5
  1.0 0.9 %copy-done.5 = f32[2,2,8,2048]{3,2,1,0:T(8,128)S(1)} copy-done((f32[2,2,8,2048]{3,2,1,0:T(8,128)S(1)}, f32[2,2,8,2048]{3,2,1,0:T(8,128)}, u32[]{:S(2)}) %copy-start.5) | copy-done | bytes 262168
  2.0 0.0 copy-start.7
  2.0 0.7 copy-done.7
  2.7 0.0 copy-start.9
  2.7 0.7 copy-done.9
  3.4 0.0 copy-start.11
  3.4 0.7 copy-done.11
  4.1 2.2 %shear.3 = bf16[16,8,32,128]{3,2,1,0:T(8,128)(2,1)S(1)} custom-call(s32[2,8]{1,0:T(2,128)S(1)} %copy-done.9, s32[2,64]{1,0:T(2,128)S(1)} %copy-done.11, f32[2,2,8,2048]{3,2,1,0:T(8,128)S(1)} %copy-done.5, bf16[2,2,256,256]{3,2,1,0:T(8,128)(2,1)S(1)} %copy-done, f32[2,16,128]{2,1,0:T(8,128)S(1)} %copy-done.7), custom_call_target="tpu_custom_call" | custom-call | tf_op jit(solution)/shard_map/shear/pallas_call | solution.py:368
  6.3 0.0 copy-start.2
  6.3 0.0 copy-start.3
  6.3 0.0 copy-start.6
  6.4 35.7 %all_to_all.10.recv = bf16[16,8,32,128]{3,2,1,0:T(8,128)(2,1)S(1)} all-to-all(bf16[16,8,32,128]{3,2,1,0:T(8,128)(2,1)S(1)} %shear.3), channel_id=1, replica_groups=mesh['grp'=16,'ln'=16] {'ln'}, dimensions={0} | all-to-all | bytes 2097152 | tf_op jit(solution)/shard_map/all_to_all | solution.py:382
  42.0 0.0 copy-done.2
  42.0 0.0 copy-done.3
  42.0 0.0 copy-done.6
  42.0 6.1 %tiles.1 = bf16[16,8,32,128]{3,2,1,0:T(8,128)(2,1)S(1)} custom-call(bf16[16,8,32,128]{3,2,1,0:T(8,128)(2,1)S(1)} %all_to_all.10.recv, f32[8,128,128]{2,1,0:T(8,128)S(1)} %bitcast.1, f32[2,128,128]{2,1,0:T(8,128)S(1)} %copy-done.6, bf16[4,2,256,256]{3,2,1,0:T(8,128)(2,1)S(1)} %copy-done.2), custom_call_target="tpu_custom_call" | custom-call | tf_op jit(solution)/shard_map/tiles/pallas_call | solution.py:384
  48.1 0.0 copy-start.1
  48.1 0.0 copy-start.4
  48.2 0.0 copy-start.8
  48.2 0.0 copy-start.10
  48.2 0.0 copy-start.12
  48.2 31.4 %all_to_all.11.recv = bf16[16,8,32,128]{3,2,1,0:T(8,128)(2,1)S(1)} all-to-all(bf16[16,8,32,128]{3,2,1,0:T(8,128)(2,1)S(1)} %tiles.1), channel_id=1, replica_groups=mesh['grp'=16,'ln'=16] {'ln'}, dimensions={0} | all-to-all | bytes 2097152 | tf_op jit(solution)/shard_map/all_to_all | solution.py:398
  79.5 0.0 copy-done.1
  79.6 0.0 copy-done.4
  79.6 0.0 copy-done.8
  79.6 0.0 copy-done.10
  79.6 0.0 copy-done.12
  79.6 2.3 %descent.1 = (f32[2,2,8,2048]{3,2,1,0:T(8,128)S(1)}, f32[4,2048]{1,0:T(4,128)S(1)}, f32[4,2048]{1,0:T(4,128)S(1)}) custom-call(s32[2,8]{1,0:T(2,128)S(1)} %copy-done.10, s32[2,64]{1,0:T(2,128)S(1)} %copy-done.12, bf16[16,8,32,128]{3,2,1,0:T(8,128)(2,1)S(1)} %all_to_all.11.recv, f32[8,2048]{1,0:T(8,128)S(1)} %copy-done.4, ...), custom_call_target="tpu_custom_call" | custom-call | tf_op jit(solution)/shard_map/descent/pallas_call | solution.py:401
  81.9 1.8 %collective-permute-start = (f32[4,2048]{1,0:T(4,128)S(1)}, f32[4,2048]{1,0:T(4,128)S(1)}, u32[]{:S(2)}, u32[]{:S(2)}) collective-permute-start(f32[4,2048]{1,0:T(4,128)S(1)} %get-tuple-element.9), channel_id=1, source_target_pairs={{0,1},{1,0},{2,3},{3,2},{4,5},{5,4},{6,7},{7,6},{8,9},{9,8},{10,11... | collective-permute-start | bytes 98312 | tf_op jit(solution)/shard_map/ppermute | solution.py:415
  83.7 3.4 %collective-permute-start.1 = (f32[4,2048]{1,0:T(4,128)S(1)}, f32[4,2048]{1,0:T(4,128)S(1)}, u32[]{:S(2)}, u32[]{:S(2)}) collective-permute-start(f32[4,2048]{1,0:T(4,128)S(1)} %get-tuple-element.10), channel_id=1, source_target_pairs={{1,2},{3,4},{5,6},{7,8},{9,10},{11,12},{13,14},{15,16},{17,18},{19... | collective-permute-start | bytes 98312 | tf_op jit(solution)/shard_map/ppermute | solution.py:414
  87.1 0.0 collective-permute-done.near
  87.1 6.0 %collective-permute-done.1.far = f32[4,2048]{1,0:T(4,128)S(1)} collective-permute-done((f32[4,2048]{1,0:T(4,128)S(1)}, f32[4,2048]{1,0:T(4,128)S(1)}, u32[]{:S(2)}, u32[]{:S(2)}) %collective-permute-start.1) | collective-permute-done | bytes 32800 | tf_op jit(solution)/shard_map/ppermute | solution.py:414
  93.1 0.8 halo.1
Async XLA Ops:
  0.0 1.0 %copy-start = (bf16[2,2,256,256]{3,2,1,0:T(8,128)(2,1)S(1)}, bf16[2,2,256,256]{3,2,1,0:T(8,128)(2,1)}, u32[]{:S(2)}) copy-start(bf16[2,2,256,256]{3,2,1,0:T(8,128)(2,1)} %constant.10.table) | copy-start | bytes 1572868
  1.0 0.9 %copy-start.5 = (f32[2,2,8,2048]{3,2,1,0:T(8,128)S(1)}, f32[2,2,8,2048]{3,2,1,0:T(8,128)}, u32[]{:S(2)}) copy-start(f32[2,2,8,2048]{3,2,1,0:T(8,128)} %obj.1) | copy-start | bytes 786436
  2.0 0.7 copy-start.7
  2.7 0.7 copy-start.9
  3.4 0.7 copy-start.11
  6.3 35.7 %copy-start.2 = (bf16[4,2,256,256]{3,2,1,0:T(8,128)(2,1)S(1)}, bf16[4,2,256,256]{3,2,1,0:T(8,128)(2,1)}, u32[]{:S(2)}) copy-start(bf16[4,2,256,256]{3,2,1,0:T(8,128)(2,1)} %constant.4.clone.table) | copy-start | bytes 3145732
  6.3 35.7 %copy-start.3 = (f32[2,4,128,128]{3,2,1,0:T(8,128)S(1)}, f32[2,4,128,128]{3,2,1,0:T(8,128)}, u32[]{:S(2)}) copy-start(f32[2,4,128,128]{3,2,1,0:T(8,128)} %param.10) | copy-start | bytes 1572868
  6.3 35.7 %copy-start.6 = (f32[2,128,128]{2,1,0:T(8,128)S(1)}, f32[2,128,128]{2,1,0:T(8,128)}, u32[]{:S(2)}) copy-start(f32[2,128,128]{2,1,0:T(8,128)} %probe.1) | copy-start | bytes 393220
  48.1 31.4 %copy-start.1 = (bf16[2,2,256,256]{3,2,1,0:T(8,128)(2,1)S(1)}, bf16[2,2,256,256]{3,2,1,0:T(8,128)(2,1)}, u32[]{:S(2)}) copy-start(bf16[2,2,256,256]{3,2,1,0:T(8,128)(2,1)} %constant.10.table) | copy-start | bytes 1572868
  48.1 31.4 %copy-start.4 = (f32[8,2048]{1,0:T(8,128)S(1)}, f32[8,2048]{1,0:T(8,128)}, u32[]{:S(2)}) copy-start(f32[8,2048]{1,0:T(8,128)} %weight.3) | copy-start | bytes 196612
  48.2 31.4 %copy-start.8 = (f32[2,16,128]{2,1,0:T(8,128)S(1)}, f32[2,16,128]{2,1,0:T(8,128)}, u32[]{:S(2)}) copy-start(f32[2,16,128]{2,1,0:T(8,128)} %constant.5.clone.tw) | copy-start | bytes 49156
  48.2 31.4 %copy-start.10 = (s32[2,8]{1,0:T(2,128)S(1)}, s32[2,8]{1,0:T(2,128)}, u32[]{:S(2)}) copy-start(s32[2,8]{1,0:T(2,128)} %shear.5) | copy-start | bytes 196
  48.2 31.4 %copy-start.12 = (s32[2,64]{1,0:T(2,128)S(1)}, s32[2,64]{1,0:T(2,128)}, u32[]{:S(2)}) copy-start(s32[2,64]{1,0:T(2,128)} %pos.3) | copy-start | bytes 1540
  81.9 5.2 %collective-permute-start = (f32[4,2048]{1,0:T(4,128)S(1)}, f32[4,2048]{1,0:T(4,128)S(1)}, u32[]{:S(2)}, u32[]{:S(2)}) collective-permute-start(f32[4,2048]{1,0:T(4,128)S(1)} %get-tuple-element.9), channel_id=1, source_target_pairs={{0,1},{1,0},{2,3},{3,2},{4,5},{5,4},{6,7},{7,6},{8,9},{9,8},{10,11... | collective-permute-start | bytes 98312 | tf_op jit(solution)/shard_map/ppermute | solution.py:415
  83.7 9.4 %collective-permute-start.1 = (f32[4,2048]{1,0:T(4,128)S(1)}, f32[4,2048]{1,0:T(4,128)S(1)}, u32[]{:S(2)}, u32[]{:S(2)}) collective-permute-start(f32[4,2048]{1,0:T(4,128)S(1)} %get-tuple-element.10), channel_id=1, source_target_pairs={{1,2},{3,4},{5,6},{7,8},{9,10},{11,12},{13,14},{15,16},{17,18},{19... | collective-permute-start | bytes 98312 | tf_op jit(solution)/shard_map/ppermute | solution.py:414

commit v2 on v1

--- a/solution.py
+++ b/solution.py
@@ -106,6 +106,16 @@
     return dot(top, high) + (dot(top, low) + dot(table[which, 1], high))
 
 
+def rmul2(x, table, which):
+    high = x.astype(BF16)
+    return dot(high, table[which, 0])
+
+
+def lmul2(table, which, x):
+    high = x.astype(BF16)
+    return dot(table[which, 0], high)
+
+
 def shear_factors(shear, tilt):
     row = lax.broadcasted_iota(jnp.int32, (ROWS, LANES), 0)
     lane = lax.broadcasted_iota(jnp.int32, (ROWS, LANES), 1)
@@ -156,7 +166,17 @@
     return small_dft(blocks, 1)
 
 
-def shear_kernel(shear, pos, obj, table, tw, out, x_ref, y_ref, z_ref, band):
+def shear_kernel(*refs):
+    given, out, x_ref, y_ref, z_ref, band = refs[:5], *refs[5:10]
+    held, sems = refs[10:15], refs[15]
+    copies = [
+        pltpu.make_async_copy(src, dst, sems.at[k]) for k, (src, dst) in enumerate(zip(given, held))
+    ]
+    for copy in copies:
+        copy.start()
+    obj, tw, table, shear, pos = held
+    copies[0].wait()
+    copies[1].wait()
     slices = obj.shape[0]
     tilts = band.shape[0]
     for s in range(slices):
@@ -164,6 +184,8 @@
             tuple(obj[s, c, :, j * LANES : (j + 1) * LANES] for c in range(2)) for j in range(OUTER)
         ]
         forward_columns(chunks, tw, x_ref, s * OUTER)
+    for copy in copies[2:]:
+        copy.wait()
     x_ref[...] = rmul(x_ref[...], table, 0)
     for t in range(tilts):
         base, powers = shear_factors(shear, t)
@@ -205,7 +227,7 @@
 
 def both(values, table, right, left):
     tile = LANES
-    halved = [rmul(jnp.concatenate(value, 1), table, right) for value in values]
+    halved = [rmul2(jnp.concatenate(value, 1), table, right) for value in values]
     stacked = [
         jnp.concatenate(
             [
@@ -216,7 +238,7 @@
         )
         for half in halved
     ]
-    full = [lmul(table, left, x) for x in stacked]
+    full = [lmul2(table, left, x) for x in stacked]
     return [
         (
             jnp.concatenate([x[:tile, :tile], x[:tile, tile:]], 0),
@@ -352,6 +374,7 @@
 
 VMEM = pl.BlockSpec(memory_space=pltpu.VMEM)
 SMEM = pl.BlockSpec(memory_space=pltpu.SMEM)
+HBM = pl.BlockSpec(memory_space=pltpu.MemorySpace.HBM)
 PARAMS = pltpu.CompilerParams(vmem_limit_bytes=24 << 20)
 
 
@@ -363,22 +386,32 @@
     depth = 2 * slices * ROWS
     table = jnp.asarray(tables())
     tw = jnp.asarray(twiddles())
+    fourier = table[:2]
     rows = slices * OUTER * ROWS
     chunk = (owners, tiles, depth, LANES)
     send = pl.pallas_call(
         shear_kernel,
         out_shape=jax.ShapeDtypeStruct(chunk, BF16),
-        in_specs=[SMEM, SMEM, VMEM, VMEM, VMEM],
+        in_specs=[HBM] * 5,
         out_specs=VMEM,
         scratch_shapes=[
             pltpu.VMEM((rows, 2 * LANES), F32),
             pltpu.VMEM((tilts * rows, 2 * LANES), F32),
             pltpu.VMEM((tilts * rows, 2 * LANES), F32),
             pltpu.VMEM((tilts, depth, COLS + LANES), F32),
+            pltpu.VMEM(object_field.shape, F32),
+            pltpu.VMEM(tw.shape, F32),
+            pltpu.VMEM(fourier.shape, BF16),
+            pltpu.SMEM(shear_steps.shape, jnp.int32),
+            pltpu.SMEM(positions.shape, jnp.int32),
+            pltpu.SemaphoreType.DMA((5,)),
         ],
         compiler_params=PARAMS,
         name="shear",
-    )(shear_steps, positions, object_field, table[:2], tw)
+    )(*[
+        pltpu.with_memory_space_constraint(x, pltpu.MemorySpace.HBM)
+        for x in (object_field, tw, fourier, shear_steps, positions)
+    ])
     recv = lax.all_to_all(send, "ln", 0, 0, tiled=True)
     group = 4
     grads = pl.pallas_call(
@@ -407,7 +440,7 @@
         + [pltpu.VMEM((tilts * rows, 2 * LANES), F32), pltpu.VMEM((rows, 2 * LANES), F32)],
         compiler_params=PARAMS,
         name="descent",
-    )(shear_steps, positions, back, smooth_weight, table[:2], tw)
+    )(shear_steps, positions, back, smooth_weight, fourier, tw)
     count = lax.axis_size("grp") * owners
     axes = ("grp", "ln")
     between = [(i, i + 1) for i in range(1, count - 1, 2)]

time: 94.2 us -> 88.2 us (0.936)
  local copies, waits for them, and re-layouts: 4.12 us -> 0.05 us
  Pallas kernels: 11.4 us -> 9.62 us
    unnamed x26 -> x16, local copies, waits for them, and re-layouts: 4.12 us -> 0.05 us
    pallas_call x1, Pallas kernels: 6.07 us -> 3.71 us  [per_device(): pl.pallas_call(tile_kernel, out_shape=jax.ShapeDtypeStruct(chunk, BF16),...]
where the time goes in v2:
time: 88.2 us; the launch traced here: 88 us
  blocking collectives  67 us (76%)
  Pallas kernels  9.62 us (11%)
  waiting for transfers between devices  5.98 us (7%)
  starting transfers between devices  5.21 us (6%)
    all_to_all x1, blocking collectives, per_device(): recv = lax.all_to_all(send, 'ln', 0, 0, tiled=True)  35.7 us
    all_to_all x1, blocking collectives, per_device(): back = lax.all_to_all(grads, 'ln', 0, 0, tiled=True)  31.4 us
    ppermute x1, waiting for transfers between devices, per_device(): far = lax.ppermute(far, axes, between + [(j, i) for i, j in between])  5.98 us
    pallas_call x1, Pallas kernels, per_device(): pl.pallas_call(tile_kernel, out_shape=jax.ShapeDtypeStruct(chunk, BF16),...  3.71 us
    ppermute x1, starting transfers between devices, per_device(): far = lax.ppermute(far, axes, between + [(j, i) for i, j in between])  3.44 us
    pallas_call x1, Pallas kernels, per_device(): pl.pallas_call(shear_kernel, out_shape=jax.ShapeDtypeStruct(chunk, BF16),...  2.87 us
    pallas_call x1, Pallas kernels, per_device(): pl.pallas_call(descent_kernel, out_shape=(whole, edge, edge), in_specs=[S...  2.28 us
  transfers between devices with their start and end apart: 2, of which 1 were waited for; matrix products, arithmetic and copies ran while one was open for 0% of the time, Pallas kernels for 0%

profile of v2, /device:TPU:4, one launch (start us, length us, event | category | flops | bytes accessed | tf_op | source)
XLA Modules:
  0.0 88.0 jit_solution(7784855808757482480)
XLA Ops:
  0.0 2.9 %shear.2 = bf16[16,8,32,128]{3,2,1,0:T(8,128)(2,1)S(1)} custom-call(f32[2,2,8,2048]{3,2,1,0:T(8,128)} %refs_0_.1, f32[2,16,128]{2,1,0:T(8,128)} %constant.5.clone.refs_1_.tw, bf16[2,2,256,256]{3,2,1,0:T(8,128)(2,1)} %constant.10.refs_2_.table, s32[2,8]{1,0:T(2,128)} %shear.3, s32[2,64]{1,0:T(2,128)} %pos.1), custom_call_target="tpu_custom_call" | custom-call | tf_op jit(solution)/shard_map/shear/pallas_call | solution.py:392
  2.9 0.0 copy-start.1
  2.9 0.0 copy-start.2
  2.9 0.0 copy-start.4
  2.9 35.7 %all_to_all.10.recv = bf16[16,8,32,128]{3,2,1,0:T(8,128)(2,1)S(1)} all-to-all(bf16[16,8,32,128]{3,2,1,0:T(8,128)(2,1)S(1)} %shear.2), channel_id=1, replica_groups=mesh['grp'=16,'ln'=16] {'ln'}, dimensions={0} | all-to-all | bytes 2097152 | tf_op jit(solution)/shard_map/all_to_all | solution.py:415
  38.6 0.0 copy-done.1
  38.6 0.0 copy-done.2
  38.6 0.0 copy-done.4
  38.6 3.7 %tiles.1 = bf16[16,8,32,128]{3,2,1,0:T(8,128)(2,1)S(1)} custom-call(bf16[16,8,32,128]{3,2,1,0:T(8,128)(2,1)S(1)} %all_to_all.10.recv, f32[8,128,128]{2,1,0:T(8,128)S(1)} %bitcast.1, f32[2,128,128]{2,1,0:T(8,128)S(1)} %copy-done.4, bf16[4,2,256,256]{3,2,1,0:T(8,128)(2,1)S(1)} %copy-done.1), custom_call_target="tpu_custom_call" | custom-call | tf_op jit(solution)/shard_map/tiles/pallas_call | solution.py:417
  42.3 0.0 copy-start
  42.3 0.0 copy-start.3
  42.3 0.0 copy-start.5
  42.4 0.0 copy-start.6
  42.4 0.0 copy-start.7
  42.4 31.4 %all_to_all.11.recv = bf16[16,8,32,128]{3,2,1,0:T(8,128)(2,1)S(1)} all-to-all(bf16[16,8,32,128]{3,2,1,0:T(8,128)(2,1)S(1)} %tiles.1), channel_id=1, replica_groups=mesh['grp'=16,'ln'=16] {'ln'}, dimensions={0} | all-to-all | bytes 2097152 | tf_op jit(solution)/shard_map/all_to_all | solution.py:431
  73.7 0.0 copy-done
  73.7 0.0 copy-done.3
  73.7 0.0 copy-done.5
  73.7 0.0 copy-done.6
  73.8 0.0 copy-done.7
  73.8 2.3 %descent.1 = (f32[2,2,8,2048]{3,2,1,0:T(8,128)S(1)}, f32[4,2048]{1,0:T(4,128)S(1)}, f32[4,2048]{1,0:T(4,128)S(1)}) custom-call(s32[2,8]{1,0:T(2,128)S(1)} %copy-done.6, s32[2,64]{1,0:T(2,128)S(1)} %copy-done.7, bf16[16,8,32,128]{3,2,1,0:T(8,128)(2,1)S(1)} %all_to_all.11.recv, f32[8,2048]{1,0:T(8,128)S(1)} %copy-done.3, bf16[2,2,256,256]{3,2,1,0:T(8,128)(2,1)S(1)} %copy-done, ...), custom_call_target="tpu_custom_call" | custom-call | tf_op jit(solution)/shard_map/descent/pallas_call | solution.py:434
  76.1 1.8 %collective-permute-start = (f32[4,2048]{1,0:T(4,128)S(1)}, f32[4,2048]{1,0:T(4,128)S(1)}, u32[]{:S(2)}, u32[]{:S(2)}) collective-permute-start(f32[4,2048]{1,0:T(4,128)S(1)} %get-tuple-element.9), channel_id=1, source_target_pairs={{0,1},{1,0},{2,3},{3,2},{4,5},{5,4},{6,7},{7,6},{8,9},{9,8},{10,11... | collective-permute-start | bytes 98312 | tf_op jit(solution)/shard_map/ppermute | solution.py:448
  77.8 3.4 %collective-permute-start.1 = (f32[4,2048]{1,0:T(4,128)S(1)}, f32[4,2048]{1,0:T(4,128)S(1)}, u32[]{:S(2)}, u32[]{:S(2)}) collective-permute-start(f32[4,2048]{1,0:T(4,128)S(1)} %get-tuple-element.10), channel_id=1, source_target_pairs={{1,2},{3,4},{5,6},{7,8},{9,10},{11,12},{13,14},{15,16},{17,18},{19... | collective-permute-start | bytes 98312 | tf_op jit(solution)/shard_map/ppermute | solution.py:447
  81.3 0.0 collective-permute-done.near
  81.3 6.0 %collective-permute-done.1.far = f32[4,2048]{1,0:T(4,128)S(1)} collective-permute-done((f32[4,2048]{1,0:T(4,128)S(1)}, f32[4,2048]{1,0:T(4,128)S(1)}, u32[]{:S(2)}, u32[]{:S(2)}) %collective-permute-start.1) | collective-permute-done | bytes 32800 | tf_op jit(solution)/shard_map/ppermute | solution.py:447
  87.3 0.8 halo.1
Async XLA Ops:
  2.9 35.7 %copy-start.1 = (bf16[4,2,256,256]{3,2,1,0:T(8,128)(2,1)S(1)}, bf16[4,2,256,256]{3,2,1,0:T(8,128)(2,1)}, u32[]{:S(2)}) copy-start(bf16[4,2,256,256]{3,2,1,0:T(8,128)(2,1)} %constant.4.clone.table) | copy-start | bytes 3145732
  2.9 35.7 %copy-start.2 = (f32[2,4,128,128]{3,2,1,0:T(8,128)S(1)}, f32[2,4,128,128]{3,2,1,0:T(8,128)}, u32[]{:S(2)}) copy-start(f32[2,4,128,128]{3,2,1,0:T(8,128)} %param.10) | copy-start | bytes 1572868
  2.9 35.7 %copy-start.4 = (f32[2,128,128]{2,1,0:T(8,128)S(1)}, f32[2,128,128]{2,1,0:T(8,128)}, u32[]{:S(2)}) copy-start(f32[2,128,128]{2,1,0:T(8,128)} %probe.1) | copy-start | bytes 393220
  42.3 31.4 %copy-start = (bf16[2,2,256,256]{3,2,1,0:T(8,128)(2,1)S(1)}, bf16[2,2,256,256]{3,2,1,0:T(8,128)(2,1)}, u32[]{:S(2)}) copy-start(bf16[2,2,256,256]{3,2,1,0:T(8,128)(2,1)} %constant.10.refs_2_.table) | copy-start | bytes 1572868
  42.3 31.4 %copy-start.3 = (f32[8,2048]{1,0:T(8,128)S(1)}, f32[8,2048]{1,0:T(8,128)}, u32[]{:S(2)}) copy-start(f32[8,2048]{1,0:T(8,128)} %weight.3) | copy-start | bytes 196612
  42.3 31.4 %copy-start.5 = (f32[2,16,128]{2,1,0:T(8,128)S(1)}, f32[2,16,128]{2,1,0:T(8,128)}, u32[]{:S(2)}) copy-start(f32[2,16,128]{2,1,0:T(8,128)} %constant.5.clone.refs_1_.tw) | copy-start | bytes 49156
  42.4 31.4 %copy-start.6 = (s32[2,8]{1,0:T(2,128)S(1)}, s32[2,8]{1,0:T(2,128)}, u32[]{:S(2)}) copy-start(s32[2,8]{1,0:T(2,128)} %shear.3) | copy-start | bytes 196
  42.4 31.4 %copy-start.7 = (s32[2,64]{1,0:T(2,128)S(1)}, s32[2,64]{1,0:T(2,128)}, u32[]{:S(2)}) copy-start(s32[2,64]{1,0:T(2,128)} %pos.1) | copy-start | bytes 1540
  76.1 5.2 %collective-permute-start = (f32[4,2048]{1,0:T(4,128)S(1)}, f32[4,2048]{1,0:T(4,128)S(1)}, u32[]{:S(2)}, u32[]{:S(2)}) collective-permute-start(f32[4,2048]{1,0:T(4,128)S(1)} %get-tuple-element.9), channel_id=1, source_target_pairs={{0,1},{1,0},{2,3},{3,2},{4,5},{5,4},{6,7},{7,6},{8,9},{9,8},{10,11... | collective-permute-start | bytes 98312 | tf_op jit(solution)/shard_map/ppermute | solution.py:448
  77.8 9.4 %collective-permute-start.1 = (f32[4,2048]{1,0:T(4,128)S(1)}, f32[4,2048]{1,0:T(4,128)S(1)}, u32[]{:S(2)}, u32[]{:S(2)}) collective-permute-start(f32[4,2048]{1,0:T(4,128)S(1)} %get-tuple-element.10), channel_id=1, source_target_pairs={{1,2},{3,4},{5,6},{7,8},{9,10},{11,12},{13,14},{15,16},{17,18},{19... | collective-permute-start | bytes 98312 | tf_op jit(solution)/shard_map/ppermute | solution.py:447

commit v3 on v2

--- a/solution.py
+++ b/solution.py
@@ -16,7 +16,8 @@
 OUTER = 16
 COLS = OUTER * LANES
 ROWS = 8
-UNROLL = 4
+UNROLL = 16
+GROUP = 4
 BF16 = jnp.bfloat16
 F32 = jnp.float32
 
@@ -249,10 +250,15 @@
 
 
 def tile_kernel(recv, measured, probe, table, out):
+    pairs = recv.shape[1] // 2
+    for q in range(0, pairs, GROUP):
+        some_pairs(range(q, min(q + GROUP, pairs)), recv, measured, probe, table, out)
+
+
+def some_pairs(pairs, recv, measured, probe, table, out):
     owners = recv.shape[0]
-    pairs = recv.shape[1] // 2
     first, second, target = [], [], []
-    for q in range(pairs):
+    for q in pairs:
         parts = [[] for _ in range(4)]
         for p in (2 * q, 2 * q + 1):
             for d in range(owners):
@@ -274,8 +280,8 @@
     grad1 = [conj_mul(w, b) for w, b in zip(wave, back)]
     back = both([conj_mul(x, b) for x, b in zip(second, back)], table, 3, 2)
     grad0 = [conj_mul(start, b) for b in back]
-    for q in range(pairs):
-        grads = (*grad0[q], *grad1[q])
+    for k, q in enumerate(pairs):
+        grads = (*grad0[k], *grad1[k])
         for p in range(2):
             for d in range(owners):
                 row = p * LANES + d * ROWS
@@ -359,7 +365,7 @@
                 far[2 * s + c : 2 * s + c + 1, cols] = jnp.where(odd, last, first)
 
 
-def halo_kernel(partial, near, far, weight, out):
+def halo_kernel(partial, far, near, weight, out):
     odd = lax.rem(lax.axis_index("ln"), 2) == 1
     row = lax.broadcasted_iota(jnp.int32, weight.shape, 0)
     near_row = jnp.where(odd, 0, ROWS - 1)
@@ -413,18 +419,11 @@
         for x in (object_field, tw, fourier, shear_steps, positions)
     ])
     recv = lax.all_to_all(send, "ln", 0, 0, tiled=True)
-    group = 4
     grads = pl.pallas_call(
         tile_kernel,
         out_shape=jax.ShapeDtypeStruct(chunk, BF16),
-        grid=(tiles // group,),
-        in_specs=[
-            pl.BlockSpec((owners, group, depth, LANES), lambda g: (0, g, 0, 0)),
-            pl.BlockSpec((group, LANES, LANES), lambda g: (g, 0, 0)),
-            pl.BlockSpec((2, LANES, LANES), lambda g: (0, 0, 0)),
-            pl.BlockSpec(table.shape, lambda g: (0, 0, 0, 0)),
-        ],
-        out_specs=pl.BlockSpec((owners, group, depth, LANES), lambda g: (0, g, 0, 0)),
+        in_specs=[VMEM] * 4,
+        out_specs=VMEM,
         compiler_params=PARAMS,
         name="tiles",
     )(recv, measured.reshape(tiles, LANES, LANES), probe_wave, table)
@@ -444,8 +443,8 @@
     count = lax.axis_size("grp") * owners
     axes = ("grp", "ln")
     between = [(i, i + 1) for i in range(1, count - 1, 2)]
+    near = lax.ppermute(near, axes, [(i, i ^ 1) for i in range(count)])
     far = lax.ppermute(far, axes, between + [(j, i) for i, j in between])
-    near = lax.ppermute(near, axes, [(i, i ^ 1) for i in range(count)])
     return pl.pallas_call(
         halo_kernel,
         out_shape=whole,
@@ -453,7 +452,7 @@
         out_specs=VMEM,
         compiler_params=PARAMS,
         name="halo",
-    )(partial, near, far, smooth_weight)
+    )(partial, far, near, smooth_weight)
 
 
 def solution(mesh):

time: 88.2 us -> 84.5 us (0.958)
  Pallas kernels: 9.62 us -> 7.67 us
  waiting for transfers between devices: 5.98 us -> 4.84 us
    ppermute x1, starting transfers between devices: 1.76 us -> 0.09 us  [per_device(): near = lax.ppermute(near, axes, [(i, i ^ 1) for i in range(count)])]
    pallas_call x1, Pallas kernels: 3.71 us -> 2.13 us  [per_device(): pl.pallas_call(tile_kernel, out_shape=jax.ShapeDtypeStruct(chunk, BF16),...]
    ppermute x1, waiting for transfers between devices: 5.98 us -> 4.83 us  [per_device(): far = lax.ppermute(far, axes, between + [(j, i) for i, j in between])]
    ppermute x1, starting transfers between devices: 3.44 us -> 4.51 us  [per_device(): far = lax.ppermute(far, axes, between + [(j, i) for i, j in between])]
where the time goes in v3:
time: 84.5 us; the launch traced here: 84.3 us
  blocking collectives  67 us (79%)
  Pallas kernels  7.67 us (9%)
  waiting for transfers between devices  4.84 us (6%)
  starting transfers between devices  4.6 us (5%)
    all_to_all x1, blocking collectives, per_device(): recv = lax.all_to_all(send, 'ln', 0, 0, tiled=True)  35.7 us
    all_to_all x1, blocking collectives, per_device(): back = lax.all_to_all(grads, 'ln', 0, 0, tiled=True)  31.4 us
    ppermute x1, waiting for transfers between devices, per_device(): far = lax.ppermute(far, axes, between + [(j, i) for i, j in between])  4.83 us
    ppermute x1, starting transfers between devices, per_device(): far = lax.ppermute(far, axes, between + [(j, i) for i, j in between])  4.51 us
    pallas_call x1, Pallas kernels, per_device(): pl.pallas_call(shear_kernel, out_shape=jax.ShapeDtypeStruct(chunk, BF16),...  2.63 us
    pallas_call x1, Pallas kernels, per_device(): pl.pallas_call(descent_kernel, out_shape=(whole, edge, edge), in_specs=[S...  2.15 us
    pallas_call x1, Pallas kernels, per_device(): pl.pallas_call(tile_kernel, out_shape=jax.ShapeDtypeStruct(chunk, BF16),...  2.13 us
  transfers between devices with their start and end apart: 2, of which 1 were waited for; matrix products, arithmetic and copies ran while one was open for 0% of the time, Pallas kernels for 0%

profile of v3, /device:TPU:4, one launch (start us, length us, event | category | flops | bytes accessed | tf_op | source)
XLA Modules:
  0.0 84.3 jit_solution(10676264626045383341)
XLA Ops:
  0.0 2.6 %shear.2 = bf16[16,8,32,128]{3,2,1,0:T(8,128)(2,1)S(1)} custom-call(f32[2,2,8,2048]{3,2,1,0:T(8,128)} %refs_0_.1, f32[2,16,128]{2,1,0:T(8,128)} %constant.5.clone.refs_1_.tw, bf16[2,2,256,256]{3,2,1,0:T(8,128)(2,1)} %constant.10.refs_2_.table, s32[2,8]{1,0:T(2,128)} %shear.3, s32[2,64]{1,0:T(2,128)} %pos.1), custom_call_target="tpu_custom_call" | custom-call | tf_op jit(solution)/shard_map/shear/pallas_call | solution.py:398
  2.6 0.0 copy-start.1
  2.7 0.0 copy-start.2
  2.7 0.0 copy-start.4
  2.7 35.7 %all_to_all.10.recv = bf16[16,8,32,128]{3,2,1,0:T(8,128)(2,1)S(1)} all-to-all(bf16[16,8,32,128]{3,2,1,0:T(8,128)(2,1)S(1)} %shear.2), channel_id=1, replica_groups=mesh['grp'=16,'ln'=16] {'ln'}, dimensions={0} | all-to-all | bytes 2097152 | tf_op jit(solution)/shard_map/all_to_all | solution.py:421
  38.4 0.0 copy-done.1
  38.4 0.0 copy-done.2
  38.4 0.0 copy-done.4
  38.4 2.1 %tiles.1 = bf16[16,8,32,128]{3,2,1,0:T(8,128)(2,1)S(1)} custom-call(bf16[16,8,32,128]{3,2,1,0:T(8,128)(2,1)S(1)} %all_to_all.10.recv, f32[8,128,128]{2,1,0:T(8,128)S(1)} %bitcast.1, f32[2,128,128]{2,1,0:T(8,128)S(1)} %copy-done.4, bf16[4,2,256,256]{3,2,1,0:T(8,128)(2,1)S(1)} %copy-done.1), custom_call_target="tpu_custom_call" | custom-call | tf_op jit(solution)/shard_map/tiles/pallas_call | solution.py:422
  40.5 0.0 copy-start
  40.5 0.0 copy-start.3
  40.5 0.0 copy-start.5
  40.5 0.0 copy-start.6
  40.6 0.0 copy-start.7
  40.6 31.4 %all_to_all.11.recv = bf16[16,8,32,128]{3,2,1,0:T(8,128)(2,1)S(1)} all-to-all(bf16[16,8,32,128]{3,2,1,0:T(8,128)(2,1)S(1)} %tiles.1), channel_id=1, replica_groups=mesh['grp'=16,'ln'=16] {'ln'}, dimensions={0} | all-to-all | bytes 2097152 | tf_op jit(solution)/shard_map/all_to_all | solution.py:430
  71.9 0.0 copy-done
  71.9 0.0 copy-done.3
  71.9 0.0 copy-done.5
  71.9 0.0 copy-done.6
  71.9 0.0 copy-done.7
  71.9 2.1 %descent.1 = (f32[2,2,8,2048]{3,2,1,0:T(8,128)S(1)}, f32[4,2048]{1,0:T(4,128)S(1)}, f32[4,2048]{1,0:T(4,128)S(1)}) custom-call(s32[2,8]{1,0:T(2,128)S(1)} %copy-done.6, s32[2,64]{1,0:T(2,128)S(1)} %copy-done.7, bf16[16,8,32,128]{3,2,1,0:T(8,128)(2,1)S(1)} %all_to_all.11.recv, f32[8,2048]{1,0:T(8,128)S(1)} %copy-done.3, bf16[2,2,256,256]{3,2,1,0:T(8,128)(2,1)S(1)} %copy-done, ...), custom_call_target="tpu_custom_call" | custom-call | tf_op jit(solution)/shard_map/descent/pallas_call | solution.py:433
  74.1 4.5 %collective-permute-start = (f32[4,2048]{1,0:T(4,128)S(1)}, f32[4,2048]{1,0:T(4,128)S(1)}, u32[]{:S(2)}, u32[]{:S(2)}) collective-permute-start(f32[4,2048]{1,0:T(4,128)S(1)} %get-tuple-element.9), channel_id=1, source_target_pairs={{1,2},{3,4},{5,6},{7,8},{9,10},{11,12},{13,14},{15,16},{17,18},{19... | collective-permute-start | bytes 98312 | tf_op jit(solution)/shard_map/ppermute | solution.py:447
  78.6 0.1 collective-permute-start.1
  78.7 4.8 %collective-permute-done.far = f32[4,2048]{1,0:T(4,128)S(1)} collective-permute-done((f32[4,2048]{1,0:T(4,128)S(1)}, f32[4,2048]{1,0:T(4,128)S(1)}, u32[]{:S(2)}, u32[]{:S(2)}) %collective-permute-start) | collective-permute-done | bytes 32800 | tf_op jit(solution)/shard_map/ppermute | solution.py:447
  83.6 0.0 collective-permute-done.1.near
  83.6 0.8 halo.1
Async XLA Ops:
  2.6 35.7 %copy-start.1 = (bf16[4,2,256,256]{3,2,1,0:T(8,128)(2,1)S(1)}, bf16[4,2,256,256]{3,2,1,0:T(8,128)(2,1)}, u32[]{:S(2)}) copy-start(bf16[4,2,256,256]{3,2,1,0:T(8,128)(2,1)} %constant.4.clone.table) | copy-start | bytes 3145732
  2.7 35.7 %copy-start.2 = (f32[2,4,128,128]{3,2,1,0:T(8,128)S(1)}, f32[2,4,128,128]{3,2,1,0:T(8,128)}, u32[]{:S(2)}) copy-start(f32[2,4,128,128]{3,2,1,0:T(8,128)} %param.10) | copy-start | bytes 1572868
  2.7 35.7 %copy-start.4 = (f32[2,128,128]{2,1,0:T(8,128)S(1)}, f32[2,128,128]{2,1,0:T(8,128)}, u32[]{:S(2)}) copy-start(f32[2,128,128]{2,1,0:T(8,128)} %probe.1) | copy-start | bytes 393220
  40.5 31.4 %copy-start = (bf16[2,2,256,256]{3,2,1,0:T(8,128)(2,1)S(1)}, bf16[2,2,256,256]{3,2,1,0:T(8,128)(2,1)}, u32[]{:S(2)}) copy-start(bf16[2,2,256,256]{3,2,1,0:T(8,128)(2,1)} %constant.10.refs_2_.table) | copy-start | bytes 1572868
  40.5 31.4 %copy-start.3 = (f32[8,2048]{1,0:T(8,128)S(1)}, f32[8,2048]{1,0:T(8,128)}, u32[]{:S(2)}) copy-start(f32[8,2048]{1,0:T(8,128)} %weight.3) | copy-start | bytes 196612
  40.5 31.4 %copy-start.5 = (f32[2,16,128]{2,1,0:T(8,128)S(1)}, f32[2,16,128]{2,1,0:T(8,128)}, u32[]{:S(2)}) copy-start(f32[2,16,128]{2,1,0:T(8,128)} %constant.5.clone.refs_1_.tw) | copy-start | bytes 49156
  40.5 31.4 %copy-start.6 = (s32[2,8]{1,0:T(2,128)S(1)}, s32[2,8]{1,0:T(2,128)}, u32[]{:S(2)}) copy-start(s32[2,8]{1,0:T(2,128)} %shear.3) | copy-start | bytes 196
  40.6 31.4 %copy-start.7 = (s32[2,64]{1,0:T(2,128)S(1)}, s32[2,64]{1,0:T(2,128)}, u32[]{:S(2)}) copy-start(s32[2,64]{1,0:T(2,128)} %pos.1) | copy-start | bytes 1540
  74.1 9.5 %collective-permute-start = (f32[4,2048]{1,0:T(4,128)S(1)}, f32[4,2048]{1,0:T(4,128)S(1)}, u32[]{:S(2)}, u32[]{:S(2)}) collective-permute-start(f32[4,2048]{1,0:T(4,128)S(1)} %get-tuple-element.9), channel_id=1, source_target_pairs={{1,2},{3,4},{5,6},{7,8},{9,10},{11,12},{13,14},{15,16},{17,18},{19... | collective-permute-start | bytes 98312 | tf_op jit(solution)/shard_map/ppermute | solution.py:447
  78.6 4.9 %collective-permute-start.1 = (f32[4,2048]{1,0:T(4,128)S(1)}, f32[4,2048]{1,0:T(4,128)S(1)}, u32[]{:S(2)}, u32[]{:S(2)}) collective-permute-start(f32[4,2048]{1,0:T(4,128)S(1)} %get-tuple-element.10), channel_id=1, source_target_pairs={{0,1},{1,0},{2,3},{3,2},{4,5},{5,4},{6,7},{7,6},{8,9},{9,8},{10,11... | collective-permute-start | bytes 98312 | tf_op jit(solution)/shard_map/ppermute | solution.py:446

commit v4 on v3

--- a/solution.py
+++ b/solution.py
@@ -228,7 +228,10 @@
 
 def both(values, table, right, left):
     tile = LANES
-    halved = [rmul2(jnp.concatenate(value, 1), table, right) for value in values]
+    rows = 2 * tile
+    flat = jnp.concatenate([jnp.concatenate(value, 1) for value in values], 0)
+    flat = rmul2(flat, table, right)
+    halved = [flat[k * rows : (k + 1) * rows] for k in range(len(values))]
     stacked = [
         jnp.concatenate(
             [
@@ -289,7 +292,7 @@
                 out[d, 2 * q + p] = mine.astype(BF16)
 
 
-def descent_kernel(shear, pos, recv, weight, table, tw, out, near, far, *scratch):
+def descent_kernel(shear, pos, recv, table, tw, out, near, far, *scratch):
     accs, (x_ref, y_ref) = scratch[:-2], scratch[-2:]
     tilts = len(accs) // 2
     per_owner = recv.shape[1] // tilts
@@ -342,13 +345,26 @@
                     value = (value[0] + before[0], value[1] + before[1])
                 put(y_ref, s * OUTER + i, value)
     y_ref[...] = rmul(y_ref[...], table, 1)
-    row = lax.broadcasted_iota(jnp.int32, (ROWS, LANES), 0)
-    lane = lax.broadcasted_iota(jnp.int32, (ROWS, LANES), 1)
     odd = lax.rem(lax.axis_index("ln"), 2) == 1
     for s in range(slices):
         chunks = inverse_columns(y_ref, s * OUTER, tw)
         for c in range(2):
-            values = [chunk[c] for chunk in chunks]
+            k = 2 * s + c
+            for j in range(OUTER):
+                v = chunks[j][c]
+                cols = slice(j * LANES, (j + 1) * LANES)
+                out[s, c, :, cols] = v
+                first, last = v[:1], v[ROWS - 1 :]
+                near[k : k + 1, cols] = jnp.where(odd, first, last)
+                far[k : k + 1, cols] = jnp.where(odd, last, first)
+
+
+def smooth_kernel(descent, weight, out):
+    row = lax.broadcasted_iota(jnp.int32, (ROWS, LANES), 0)
+    lane = lax.broadcasted_iota(jnp.int32, (ROWS, LANES), 1)
+    for s in range(out.shape[0]):
+        for c in range(2):
+            values = [descent[s, c, :, j * LANES : (j + 1) * LANES] for j in range(OUTER)]
             ahead = [pltpu.roll(v, 1, 1) for v in values]
             behind = [pltpu.roll(v, LANES - 1, 1) for v in values]
             for j in range(OUTER):
@@ -360,9 +376,6 @@
                 below = jnp.where(row == ROWS - 1, 0.0, pltpu.roll(v, ROWS - 1, 0))
                 around = (above + below) + (left + right)
                 out[s, c, :, cols] = v + weight[:, cols] * (around - 4.0 * v)
-                first, last = v[:1], v[ROWS - 1 :]
-                near[2 * s + c : 2 * s + c + 1, cols] = jnp.where(odd, first, last)
-                far[2 * s + c : 2 * s + c + 1, cols] = jnp.where(odd, last, first)
 
 
 def halo_kernel(partial, far, near, weight, out):
@@ -430,21 +443,30 @@
     back = lax.all_to_all(grads, "ln", 0, 0, tiled=True)
     edge = jax.ShapeDtypeStruct((2 * slices, COLS), F32)
     whole = jax.ShapeDtypeStruct((slices, 2, ROWS, COLS), F32)
-    partial, near, far = pl.pallas_call(
+    descent, near, far = pl.pallas_call(
         descent_kernel,
         out_shape=(whole, edge, edge),
-        in_specs=[SMEM, SMEM, VMEM, VMEM, VMEM, VMEM],
+        in_specs=[SMEM, SMEM, VMEM, VMEM, VMEM],
         out_specs=(VMEM, VMEM, VMEM),
         scratch_shapes=[pltpu.VMEM((depth, COLS + LANES), F32) for _ in range(2 * tilts)]
         + [pltpu.VMEM((tilts * rows, 2 * LANES), F32), pltpu.VMEM((rows, 2 * LANES), F32)],
         compiler_params=PARAMS,
         name="descent",
-    )(shear_steps, positions, back, smooth_weight, fourier, tw)
+    )(shear_steps, positions, back, fourier, tw)
     count = lax.axis_size("grp") * owners
     axes = ("grp", "ln")
     between = [(i, i + 1) for i in range(1, count - 1, 2)]
     near = lax.ppermute(near, axes, [(i, i ^ 1) for i in range(count)])
     far = lax.ppermute(far, axes, between + [(j, i) for i, j in between])
+    partial = pl.pallas_call(
+        smooth_kernel,
+        out_shape=whole,
+        in_specs=[VMEM] * 2,
+        out_specs=VMEM,
+        compiler_params=PARAMS,
+        cost_estimate=pl.CostEstimate(flops=1 << 22, bytes_accessed=1 << 20, transcendentals=0),
+        name="smooth",
+    )(descent, smooth_weight)
     return pl.pallas_call(
         halo_kernel,
         out_shape=whole,

time: 84.5 us -> 84.1 us (level)
  no operation moved by 1% of the time
where the time goes in v4:
time: 84.1 us; the launch traced here: 83.9 us
  blocking collectives  67 us (80%)
  Pallas kernels  7.47 us (9%)
  starting transfers between devices  4.6 us (5%)
  waiting for transfers between devices  4.6 us (5%)
    all_to_all x1, blocking collectives, per_device(): recv = lax.all_to_all(send, 'ln', 0, 0, tiled=True)  35.7 us
    all_to_all x1, blocking collectives, per_device(): back = lax.all_to_all(grads, 'ln', 0, 0, tiled=True)  31.4 us
    ppermute x1, waiting for transfers between devices, per_device(): far = lax.ppermute(far, axes, between + [(j, i) for i, j in between])  4.6 us
    ppermute x1, starting transfers between devices, per_device(): far = lax.ppermute(far, axes, between + [(j, i) for i, j in between])  4.51 us
    pallas_call x1, Pallas kernels, per_device(): pl.pallas_call(shear_kernel, out_shape=jax.ShapeDtypeStruct(chunk, BF16),...  2.63 us
    pallas_call x1, Pallas kernels, per_device(): pl.pallas_call(descent_kernel, out_shape=(whole, edge, edge), in_specs=[S...  2.03 us
    pallas_call x1, Pallas kernels, per_device(): pl.pallas_call(tile_kernel, out_shape=jax.ShapeDtypeStruct(chunk, BF16),...  1.83 us
  transfers between devices with their start and end apart: 2, of which 1 were waited for; matrix products, arithmetic and copies ran while one was open for 0% of the time, Pallas kernels for 0%

profile of v4, /device:TPU:4, one launch (start us, length us, event | category | flops | bytes accessed | tf_op | source)
XLA Modules:
  0.0 83.9 jit_solution(5052385208922689261)
XLA Ops:
  0.0 2.6 %shear.2 = bf16[16,8,32,128]{3,2,1,0:T(8,128)(2,1)S(1)} custom-call(f32[2,2,8,2048]{3,2,1,0:T(8,128)} %refs_0_.1, f32[2,16,128]{2,1,0:T(8,128)} %constant.5.clone.refs_1_.tw, bf16[2,2,256,256]{3,2,1,0:T(8,128)(2,1)} %constant.10.refs_2_.table, s32[2,8]{1,0:T(2,128)} %shear.3, s32[2,64]{1,0:T(2,128)} %pos.1), custom_call_target="tpu_custom_call" | custom-call | tf_op jit(solution)/shard_map/shear/pallas_call | solution.py:411
  2.6 0.0 copy-start.1
  2.7 0.0 copy-start.2
  2.7 0.0 copy-start.4
  2.7 35.7 %all_to_all.10.recv = bf16[16,8,32,128]{3,2,1,0:T(8,128)(2,1)S(1)} all-to-all(bf16[16,8,32,128]{3,2,1,0:T(8,128)(2,1)S(1)} %shear.2), channel_id=1, replica_groups=mesh['grp'=16,'ln'=16] {'ln'}, dimensions={0} | all-to-all | bytes 2097152 | tf_op jit(solution)/shard_map/all_to_all | solution.py:434
  38.4 0.0 copy-done.1
  38.4 0.0 copy-done.2
  38.4 0.0 copy-done.4
  38.4 1.8 %tiles.1 = bf16[16,8,32,128]{3,2,1,0:T(8,128)(2,1)S(1)} custom-call(bf16[16,8,32,128]{3,2,1,0:T(8,128)(2,1)S(1)} %all_to_all.10.recv, f32[8,128,128]{2,1,0:T(8,128)S(1)} %bitcast.1, f32[2,128,128]{2,1,0:T(8,128)S(1)} %copy-done.4, bf16[4,2,256,256]{3,2,1,0:T(8,128)(2,1)S(1)} %copy-done.1), custom_call_target="tpu_custom_call" | custom-call | tf_op jit(solution)/shard_map/tiles/pallas_call | solution.py:435
  40.2 0.0 copy-start
  40.2 0.0 copy-start.5
  40.2 0.0 copy-start.6
  40.2 0.0 copy-start.7
  40.3 31.4 %all_to_all.11.recv = bf16[16,8,32,128]{3,2,1,0:T(8,128)(2,1)S(1)} all-to-all(bf16[16,8,32,128]{3,2,1,0:T(8,128)(2,1)S(1)} %tiles.1), channel_id=1, replica_groups=mesh['grp'=16,'ln'=16] {'ln'}, dimensions={0} | all-to-all | bytes 2097152 | tf_op jit(solution)/shard_map/all_to_all | solution.py:443
  71.6 0.0 copy-done
  71.6 0.0 copy-done.5
  71.6 0.0 copy-done.6
  71.6 0.0 copy-done.7
  71.6 0.0 copy-start.3
  71.6 2.0 %descent.1 = (f32[2,2,8,2048]{3,2,1,0:T(8,128)S(1)}, f32[4,2048]{1,0:T(4,128)S(1)}, f32[4,2048]{1,0:T(4,128)S(1)}) custom-call(s32[2,8]{1,0:T(2,128)S(1)} %copy-done.6, s32[2,64]{1,0:T(2,128)S(1)} %copy-done.7, bf16[16,8,32,128]{3,2,1,0:T(8,128)(2,1)S(1)} %all_to_all.11.recv, bf16[2,2,256,256]{3,2,1,0:T(8,128)(2,1)S(1)} %copy-done, f32[2,16,128]{2,1,0:T(8,128)S(1)} %copy-done.5), custom_call_target="tpu_custom_call" | custom-call | tf_op jit(solution)/shard_map/descent/pallas_call | solution.py:446
  73.7 4.5 %collective-permute-start = (f32[4,2048]{1,0:T(4,128)S(1)}, f32[4,2048]{1,0:T(4,128)S(1)}, u32[]{:S(2)}, u32[]{:S(2)}) collective-permute-start(f32[4,2048]{1,0:T(4,128)S(1)} %get-tuple-element.9), channel_id=1, source_target_pairs={{1,2},{3,4},{5,6},{7,8},{9,10},{11,12},{13,14},{15,16},{17,18},{19... | collective-permute-start | bytes 98312 | tf_op jit(solution)/shard_map/ppermute | solution.py:460
  78.2 0.1 collective-permute-start.1
  78.3 0.0 copy-done.3
  78.3 0.2 smooth.1.partial
  78.5 4.6 %collective-permute-done.far = f32[4,2048]{1,0:T(4,128)S(1)} collective-permute-done((f32[4,2048]{1,0:T(4,128)S(1)}, f32[4,2048]{1,0:T(4,128)S(1)}, u32[]{:S(2)}, u32[]{:S(2)}) %collective-permute-start) | collective-permute-done | bytes 32800 | tf_op jit(solution)/shard_map/ppermute | solution.py:460
  83.1 0.0 collective-permute-done.1.near
  83.1 0.8 halo.1
Async XLA Ops:
  2.6 35.7 %copy-start.1 = (bf16[4,2,256,256]{3,2,1,0:T(8,128)(2,1)S(1)}, bf16[4,2,256,256]{3,2,1,0:T(8,128)(2,1)}, u32[]{:S(2)}) copy-start(bf16[4,2,256,256]{3,2,1,0:T(8,128)(2,1)} %constant.4.clone.table) | copy-start | bytes 3145732
  2.7 35.7 %copy-start.2 = (f32[2,4,128,128]{3,2,1,0:T(8,128)S(1)}, f32[2,4,128,128]{3,2,1,0:T(8,128)}, u32[]{:S(2)}) copy-start(f32[2,4,128,128]{3,2,1,0:T(8,128)} %param.10) | copy-start | bytes 1572868
  2.7 35.7 %copy-start.4 = (f32[2,128,128]{2,1,0:T(8,128)S(1)}, f32[2,128,128]{2,1,0:T(8,128)}, u32[]{:S(2)}) copy-start(f32[2,128,128]{2,1,0:T(8,128)} %probe.1) | copy-start | bytes 393220
  40.2 31.4 %copy-start = (bf16[2,2,256,256]{3,2,1,0:T(8,128)(2,1)S(1)}, bf16[2,2,256,256]{3,2,1,0:T(8,128)(2,1)}, u32[]{:S(2)}) copy-start(bf16[2,2,256,256]{3,2,1,0:T(8,128)(2,1)} %constant.10.refs_2_.table) | copy-start | bytes 1572868
  40.2 31.4 %copy-start.5 = (f32[2,16,128]{2,1,0:T(8,128)S(1)}, f32[2,16,128]{2,1,0:T(8,128)}, u32[]{:S(2)}) copy-start(f32[2,16,128]{2,1,0:T(8,128)} %constant.5.clone.refs_1_.tw) | copy-start | bytes 49156
  40.2 31.4 %copy-start.6 = (s32[2,8]{1,0:T(2,128)S(1)}, s32[2,8]{1,0:T(2,128)}, u32[]{:S(2)}) copy-start(s32[2,8]{1,0:T(2,128)} %shear.3) | copy-start | bytes 196
  40.2 31.4 %copy-start.7 = (s32[2,64]{1,0:T(2,128)S(1)}, s32[2,64]{1,0:T(2,128)}, u32[]{:S(2)}) copy-start(s32[2,64]{1,0:T(2,128)} %pos.1) | copy-start | bytes 1540
  71.6 6.7 %copy-start.3 = (f32[8,2048]{1,0:T(8,128)S(1)}, f32[8,2048]{1,0:T(8,128)}, u32[]{:S(2)}) copy-start(f32[8,2048]{1,0:T(8,128)} %weight.3) | copy-start | bytes 196612
  73.7 9.5 %collective-permute-start = (f32[4,2048]{1,0:T(4,128)S(1)}, f32[4,2048]{1,0:T(4,128)S(1)}, u32[]{:S(2)}, u32[]{:S(2)}) collective-permute-start(f32[4,2048]{1,0:T(4,128)S(1)} %get-tuple-element.9), channel_id=1, source_target_pairs={{1,2},{3,4},{5,6},{7,8},{9,10},{11,12},{13,14},{15,16},{17,18},{19... | collective-permute-start | bytes 98312 | tf_op jit(solution)/shard_map/ppermute | solution.py:460
  78.2 4.9 %collective-permute-start.1 = (f32[4,2048]{1,0:T(4,128)S(1)}, f32[4,2048]{1,0:T(4,128)S(1)}, u32[]{:S(2)}, u32[]{:S(2)}) collective-permute-start(f32[4,2048]{1,0:T(4,128)S(1)} %get-tuple-element.10), channel_id=1, source_target_pairs={{0,1},{1,0},{2,3},{3,2},{4,5},{5,4},{6,7},{7,6},{8,9},{9,8},{10,11... | collective-permute-start | bytes 98312 | tf_op jit(solution)/shard_map/ppermute | solution.py:459
